TPU v7x, 32 devices: a whole 2x2x4 slice. The times are simulated.
32 devices in a mesh: dp: 4 (over y, core), space: 8 (over z, x).
Axes of the slice: x: 2, y: 2, z: 4, core: 2. Of those that a mesh axis runs over, the one named last changes fastest.
Arguments:
- activations: bfloat16 [2, 4, 8, 16, 32, 768], P(None, 'dp', None, 'space'), may hold values from -60 to 60
- out_grads: bfloat16 [2, 4, 8, 16, 32, 768], P(None, 'dp', None, 'space'), may hold values from -6 to 6
- omega: bfloat16 [768, 128], replicated, may hold values from -0.21875 to 0.21875
Outputs:
- basis: float32 [2, 20736, 128], P(None, ('dp', 'space'))
All inputs are finite; a program needn't handle non-finite values.
Results may differ from a plain program's by a relative error of at most 0.0033.
Values may be sent and summed in bfloat16 or wider, within the bound.
No kernel may reach another device: no remote copies, remote signals or barrier semaphores. Data moves between devices by JAX's collectives and lax.ppermute only.
A program may use at most 128 MiB of HBM per device.

v0:
```python
import functools
import math

import jax
import jax.numpy as jnp
import numpy as np
from jax import lax
from jax.experimental import pallas as pl
from jax.experimental.pallas import tpu as pltpu
from jax.sharding import PartitionSpec as P


AXES = ("dp", "space")
F32, BF16 = jnp.float32, jnp.bfloat16
HIGHEST = lax.Precision.HIGHEST


def swap(value, mask, total):
    return lax.ppermute(value, AXES, [(d, d ^ mask) for d in range(total)])


def halo(value, axis, dim):
    count, length = lax.axis_size(axis), value.shape[dim]
    up = [(i, i + 1) for i in range(count - 1)]
    before = lax.ppermute(lax.slice_in_dim(value, length - 1, length, axis=dim), axis, up)
    after = lax.ppermute(lax.slice_in_dim(value, 0, 1, axis=dim), axis, [(j, i) for i, j in up])
    return jnp.concatenate([before, value, after], axis=dim)


def product_kernel(frames, height, widths, rank, act_ref, sk_ref, out_ref, act_t, wide):
    step = pl.program_id(0)

    @pl.when(step == 0)
    def _():
        act_t[...] = act_ref[...].T
        zero = jnp.zeros((height + 2, widths, 3 * rank), BF16)
        wide[0] = zero
        wide[frames + 1] = zero
        rows = frames * (height + 2) * widths
        flat = sk_ref[...].astype(F32).reshape(rows, rank)
        at = lax.rem(lax.broadcasted_iota(jnp.int32, (rows, rank), 0), widths)
        later = jnp.where(at == widths - 1, 0.0, pltpu.roll(flat, rows - 1, 0))
        earlier = jnp.where(at == 0, 0.0, pltpu.roll(flat, 1, 0))
        shape = (frames, height + 2, widths, rank)
        wide[1 : frames + 1, :, :, 0:rank] = later.astype(BF16).reshape(shape)
        wide[1 : frames + 1, :, :, rank : 2 * rank] = sk_ref[...]
        wide[1 : frames + 1, :, :, 2 * rank :] = earlier.astype(BF16).reshape(shape)

    along_t, along_h = step // 3, lax.rem(step, 3)
    window = wide[pl.ds(2 - along_t, frames), pl.ds(2 - along_h, height)]
    window = window.reshape(frames * height * widths, 3 * rank)
    made = jnp.dot(act_t[...], window, preferred_element_type=F32)
    for c in range(3):
        out_ref[c] = made[:, c * rank : (c + 1) * rank]


def product(act, extended):
    frames, rows, widths, rank = extended.shape
    height, channels = rows - 2, act.shape[-1]
    positions = frames * height * widths
    return pl.pallas_call(
        functools.partial(product_kernel, frames, height, widths, rank),
        grid=(9,),
        in_specs=[
            pl.BlockSpec((positions, channels), lambda s: (0, 0)),
            pl.BlockSpec((frames, rows, widths, rank), lambda s: (0, 0, 0, 0)),
        ],
        out_specs=pl.BlockSpec((3, channels, rank), lambda s: (s, 0, 0)),
        out_shape=jax.ShapeDtypeStruct((27, channels, rank), F32),
        scratch_shapes=[
            pltpu.VMEM((channels, positions), BF16),
            pltpu.VMEM((frames + 2, rows, widths, 3 * rank), BF16),
        ],
        compiler_params=pltpu.CompilerParams(vmem_limit_bytes=40 * 2**20),
        cost_estimate=pl.CostEstimate(
            flops=2 * 27 * positions * channels * rank,
            bytes_accessed=27 * channels * rank * 4 + positions * channels * 2,
            transcendentals=0,
        ),
        name="product",
    )(act.reshape(positions, channels), extended)


def three(value):
    one = value.astype(BF16).astype(F32)
    two = (value - one).astype(BF16).astype(F32)
    return one, two, value - one - two


def outer(left, right):
    a, b, c = three(left)
    d, e, f = three(right)
    lhs = jnp.concatenate([a, a, b, a, b, c], axis=0).astype(BF16)
    rhs = jnp.concatenate([d, e, d, f, e, d], axis=0).astype(BF16)
    return lax.dot_general(lhs, rhs, (((0,), (0,)), ((), ())), preferred_element_type=F32)


def eliminate(grams, works, put):
    size = grams[0].shape[0]
    eye = lax.broadcasted_iota(jnp.int32, (size, size), 0) == lax.broadcasted_iota(jnp.int32, (size, size), 1)
    count = range(len(grams))
    for i in count:
        works[i][:, :size] = grams[i]
        works[i][:, size:] = eye.astype(F32)
    sub = lax.broadcasted_iota(jnp.int32, (8, 1), 0)
    for start in range(0, size, 8):
        rows = [works[i][start : start + 8, :] for i in count]
        cols = [
            [jnp.broadcast_to(rows[i][:, start + r : start + r + 1], (8, size)) for r in range(8)] for i in count
        ]
        for r in range(8):
            for i in count:
                scale = lax.rsqrt(cols[i][r][r : r + 1, :])
                below = jnp.where(sub > r, cols[i][r] * scale, 0.0)
                for c in range(r + 1, 8):
                    cols[i][c] = cols[i][c] - below * (cols[i][c][r : r + 1, :] * scale)
                row = rows[i][r : r + 1, :] * jnp.concatenate([scale, scale], axis=1)
                rest = rows[i] - jnp.concatenate([below, below], axis=1) * row
                rows[i] = jnp.where(sub == r, row, rest)
        for i in count:
            put(i, start, rows[i][:, size:])
            if start + 8 < size:
                update = outer(rows[i][:, :size], rows[i])
                works[i][start + 8 :, :] = works[i][start + 8 :, :] - update[start + 8 :, :]


def inverse_kernel(gram_ref, out_ref, work):
    def put(i, start, value):
        out_ref[start : start + 8, :] = value

    eliminate([gram_ref[...]], [work], put)


def inverse_of_factor(gram):
    size = gram.shape[-1]
    return pl.pallas_call(
        inverse_kernel,
        out_shape=jax.ShapeDtypeStruct((size, size), F32),
        scratch_shapes=[pltpu.VMEM((size, 2 * size), F32)],
        compiler_params=pltpu.CompilerParams(vmem_limit_bytes=4 * 2**20),
        name="inverse",
    )(gram)


def finish_kernel(size, scale, gram_ref, first_ref, second_ref, out_ref, one, two, high, middle, low):
    down = lax.broadcasted_iota(jnp.int32, (size, size), 0)
    across = lax.broadcasted_iota(jnp.int32, (size, size), 1)
    packed = gram_ref[0:size, :]
    under = jnp.where(down > across, packed, 0.0)
    first = under + under.T + jnp.where(down == across, gram_ref[size : size + 1, :], 0.0)
    second = jnp.where(down <= across, packed, jnp.where(down < across, packed, 0.0).T)

    def put(i, start, value):
        for ref, part in zip((high, middle, low), three(value)):
            ref[i, start : start + 8, :] = part

    eliminate([first, second], [one, two], put)
    for i, ref in enumerate((first_ref, second_ref)):
        d, e, f = (part[i].astype(BF16) for part in (high, middle, low))
        rhs = jnp.concatenate([d, e, d, f, e, d], axis=1)
        made = lax.dot_general(ref[...], rhs, (((1,), (1,)), ((), ())), preferred_element_type=F32)
        out_ref[i] = made * scale


def finish(packed, first, second, scale):
    size = packed.shape[-1]
    return pl.pallas_call(
        functools.partial(finish_kernel, size, scale),
        out_shape=jax.ShapeDtypeStruct((2, first.shape[0], size), F32),
        scratch_shapes=[pltpu.VMEM((size, 2 * size), F32)] * 2 + [pltpu.VMEM((2, size, size), F32)] * 3,
        compiler_params=pltpu.CompilerParams(vmem_limit_bytes=8 * 2**20),
        cost_estimate=pl.CostEstimate(flops=2**31, bytes_accessed=2**22, transcendentals=0),
        name="finish",
    )(packed, first, second)


def pick(value, index, axis):
    return lax.dynamic_index_in_dim(value, index, axis, keepdims=False)


def halve(value, axis, own, mask, total):
    sent = pick(value, 1 - own, axis).astype(BF16)
    return pick(value, own, axis) + swap(sent, mask, total).astype(F32)


def scatter_layer(partial, bits, total):
    rank = partial.shape[-1]
    rows = partial.shape[0] * partial.shape[1] // total
    count = len(bits)
    core_at = count - 1 - (lax.axis_size("space").bit_length() - 1)
    view = partial.reshape((2,) * count + (rows, rank))
    masks = [1 << (count - 1 - i) for i in range(count)]
    if count == 5 and core_at == 1:
        y, _, zh, zl, x = bits
        my, mc, _, mzl, mx = masks
        view = halve(view, 1, bits[1], mc, total)
        one, two = view[:, 0], view[:, 1]
        one = halve(one, 2, x, mx, total)
        two = halve(two, 0, y, my, total)
        one = halve(one, 0, y, my, total)
        two = halve(two, 1, x, mx, total)
        z = 2 * zh + zl
        both = jnp.stack([one, two]).reshape(4, rows, rank)
        got = [swap(pick(both, z ^ m, 0).astype(BF16), m * mzl, total) for m in (1, 2, 3)]
        return pick(both, z, 0) + (got[0].astype(F32) + got[1].astype(F32) + got[2].astype(F32))
    order = [core_at] + [i for i in range(count) if i != core_at]
    left = list(range(count))
    for i in order:
        view = halve(view, left.index(i), bits[i], masks[i], total)
        left.remove(i)
    return view


def shards(activations, out_grads, omega):
    layer_count, _, frames, height, widths, channels = activations.shape
    rank = omega.shape[1]
    total = lax.axis_size("dp") * lax.axis_size("space")
    count = total.bit_length() - 1
    me = lax.axis_index("dp") * lax.axis_size("space") + lax.axis_index("space")
    bits = [(me >> (count - 1 - i)) & 1 for i in range(count)]
    core_mask = lax.axis_size("space")
    core = lax.axis_index("dp") & 1

    sketched = jnp.dot(out_grads.reshape(-1, channels), omega, preferred_element_type=F32).astype(BF16)
    sketched = sketched.reshape(layer_count, frames, height, widths, rank)
    extended = halo(sketched, "space", 2)
    blocks = []
    for layer in range(layer_count):
        partial = product(activations[layer], extended[layer])
        blocks.append(scatter_layer(partial, bits, total))
    rows = jnp.stack(blocks)
    gram = jnp.einsum("lnr,lns->lrs", rows, rows, precision=HIGHEST)
    mine = pick(gram, core, 0) + swap(pick(gram, 1 - core, 0), core_mask, total)
    for i in range(count):
        mask = 1 << i
        if mask != core_mask:
            mine = mine + swap(mine, mask, total)
    inverse = inverse_of_factor(mine)
    other = swap(inverse, core_mask, total)
    inverses = [jnp.where(core == layer, inverse, other) for layer in range(2)]
    scale = math.sqrt(27 * channels)
    basis = [jnp.dot(rows[i], inverses[i].T, precision=HIGHEST) * scale for i in range(2)]
    return jnp.stack(basis)


UNITS = 28
PLACE, BY_Z, BY_CHIP, FINAL = 0, 3, 3 + 4 * UNITS, 3 + 4 * UNITS + 32


@functools.lru_cache
def unit_tables():
    table = np.zeros((32, FINAL + 27), np.int32)
    for device in range(32):
        y, core, z, x = device >> 4, (device >> 3) & 1, (device >> 1) & 3, device & 1
        quarter = 2 * y + x
        first = 16 * core + 4 * quarter

        def units_for(target):
            return [4 * k + s for k in range(27) for s in range(4) if ((32 * k + first + s) // 54) % 4 == target]

        row = [core, x, quarter]
        for m in range(4):
            units = units_for(z ^ m)
            row += units + [108] * (UNITS - len(units))
        held = units_for(z)
        for m in range(4):
            for other in range(2):
                q = quarter ^ m
                target = ((q >> 1) << 4) | ((core ^ other) << 3) | (z << 1) | (q & 1)
                for s in range(4):
                    found = [p for p, n in enumerate(held) if n % 4 == s and (8 * (n - s) + first + s) // 27 == target]
                    row.append(found[0] if found else UNITS)
        for v in range(27):
            column = (27 * device + v) % 32
            row.append(16 * ((column // 16) ^ core) + 4 * (((column % 16) // 4) ^ quarter) + column % 4)
        table[device] = row
    return table


def turn_kernel(frames, chunk, half, table_ref, own_ref, got_ref, p0, p1, p2, p3, work):
    at = pl.multiple_of(table_ref[PLACE] * half, 128)
    quarter = table_ref[PLACE + 2]
    each = half // 4
    for t in range(frames):
        rows = slice(chunk * t, chunk * (t + 1))
        block = jnp.concatenate([own_ref[rows, pl.ds(at, half)], got_ref[rows, pl.ds(at, half)]], axis=0)
        work[:, :, 2 * chunk * t : 2 * chunk * (t + 1)] = block.T.reshape(4, each, 2 * chunk)
    for m, ref in enumerate((p0, p1, p2, p3)):
        ref[...] = work[quarter ^ m]


def limit(mib):
    return pltpu.CompilerParams(vmem_limit_bytes=mib * 2**20)


def turn(table, own, got, layer, frames):
    positions, half = own.shape[1], own.shape[2] // 2
    vmem = pl.BlockSpec(memory_space=pltpu.VMEM)
    return pl.pallas_call(
        functools.partial(turn_kernel, frames, positions // frames, half),
        grid=(1,),
        in_specs=[
            pl.BlockSpec(memory_space=pltpu.SMEM),
            pl.BlockSpec((None, positions, own.shape[2]), lambda i: (layer, 0, 0)),
            pl.BlockSpec((None, positions, own.shape[2]), lambda i: (layer, 0, 0)),
        ],
        out_specs=[vmem] * 4,
        out_shape=[jax.ShapeDtypeStruct((half // 4, 2 * positions), BF16)] * 4,
        scratch_shapes=[pltpu.VMEM((4, half // 4, 2 * positions), BF16)],
        compiler_params=limit(10),
        cost_estimate=pl.CostEstimate(flops=0, bytes_accessed=8 * positions * half, transcendentals=0),
        name="turn",
    )(table, own, got)


def pieces_kernel(table_ref, sketched_ref, edge_ref, *outs):
    x = table_ref[PLACE + 1]
    for layer, out_ref in enumerate(outs):
        out_ref[:, pl.ds(1 - x, 2)] = sketched_ref[layer]
        out_ref[:, pl.ds(2 * x, 1)] = edge_ref[layer]


def pieces_of(table, sketched, edge):
    _, frames, height, widths, rank = sketched.shape
    vmem = pl.BlockSpec(memory_space=pltpu.VMEM)
    return pl.pallas_call(
        pieces_kernel,
        in_specs=[pl.BlockSpec(memory_space=pltpu.SMEM), vmem, vmem],
        out_specs=[vmem] * 2,
        out_shape=[jax.ShapeDtypeStruct((frames, height + 1, widths, rank), BF16)] * 2,
        compiler_params=limit(4),
        cost_estimate=pl.CostEstimate(flops=0, bytes_accessed=2**20, transcendentals=0),
        name="pieces",
    )(table, sketched, edge)


def plane_kernel(frames, widths, rank, table_ref, *refs):
    acts, sides, refs = refs[:4], (refs[4:8], refs[8:12]), refs[12:]
    keep_ref, s1, s2, s3, lhs, wide, acc, units = refs
    x = table_ref[PLACE + 1]
    each, depth = acts[0].shape
    frame = depth // frames
    for m, ref in enumerate(acts):
        value = ref[...]
        zero = jnp.zeros((each, frame), BF16)
        lhs[m, 0:each, 0:frame] = zero
        lhs[m, 0:each, frame:] = value[:, : depth - frame]
        lhs[m, each : 2 * each, :] = value
        lhs[m, 2 * each :, : depth - frame] = value[:, frame:]
        lhs[m, 2 * each :, depth - frame :] = zero
    rows = frames * 3 * widths
    at = lax.rem(lax.broadcasted_iota(jnp.int32, (rows, rank), 0), widths)
    for side, pieces in enumerate(sides):
        for m in range(4):
            piece = pieces[m][...]
            to = pl.ds(3 * (x ^ (m & 1)), 3)
            flat = piece.astype(F32).reshape(rows, rank)
            later = jnp.where(at == widths - 1, 0.0, pltpu.roll(flat, rows - 1, 0))
            earlier = jnp.where(at == 0, 0.0, pltpu.roll(flat, 1, 0))
            wide[m >> 1, :, side, to, :, 0:rank] = later.astype(BF16).reshape(piece.shape)
            wide[m >> 1, :, side, to, :, rank : 2 * rank] = piece
            wide[m >> 1, :, side, to, :, 2 * rank :] = earlier.astype(BF16).reshape(piece.shape)

    blocks = each // 24
    units[27 * blocks] = jnp.zeros((24, rank), F32)

    @pl.loop(0, 3)
    def _(along_h):
        for m in range(4):
            window = wide[m >> 1, :, :, pl.ds(2 * (x ^ (m & 1)) + 2 - along_h, 2)]
            made = jnp.dot(lhs[m], window.reshape(depth, 3 * rank), preferred_element_type=F32)
            acc[...] = made if m == 0 else acc[...] + made
        for a in range(3):
            for c in range(3):
                part = acc[a * each : (a + 1) * each, c * rank : (c + 1) * rank]
                units[pl.ds((9 * a + 3 * along_h + c) * blocks, blocks)] = part.reshape(blocks, 24, rank)

    @pl.loop(0, UNITS)
    def _(p):
        keep_ref[p] = units[table_ref[BY_Z + p]]
        for m, ref in enumerate((s1, s2, s3)):
            ref[p] = units[table_ref[BY_Z + (m + 1) * UNITS + p]].astype(BF16)


def plane(table, act, got, own, other):
    frames, _, widths, rank = own[0].shape
    each, depth = act.shape
    vmem = pl.BlockSpec(memory_space=pltpu.VMEM)
    smem = pl.BlockSpec(memory_space=pltpu.SMEM)
    return pl.pallas_call(
        functools.partial(plane_kernel, frames, widths, rank),
        in_specs=[smem] + [vmem] * 12,
        out_specs=[vmem] * 4,
        out_shape=[jax.ShapeDtypeStruct((UNITS, 24, rank), F32)]
        + [jax.ShapeDtypeStruct((UNITS, 24, rank), BF16)] * 3,
        scratch_shapes=[
            pltpu.VMEM((4, 3 * each, depth), BF16),
            pltpu.VMEM((2, frames, 2, 6, widths, 3 * rank), BF16),
            pltpu.VMEM((3 * each, 3 * rank), F32),
            pltpu.VMEM((27 * each // 24 + 1, 24, rank), F32),
        ],
        compiler_params=limit(18),
        cost_estimate=pl.CostEstimate(
            flops=2 * 27 * 4 * depth * each * rank, bytes_accessed=6 * 2**20, transcendentals=0
        ),
        name="plane",
    )(table, act, *got, *own, *other)


def gather_kernel(rank, joined, table_ref, *refs):
    (keep_ref, g1, g2, g3), refs = refs[:4], refs[4:]
    first_ref, refs = (refs[0], refs[1:]) if joined else (None, refs)
    gram_ref, slots, rows = refs[0], refs[1:5], refs[5]
    total = keep_ref[...] + (g1[...].astype(F32) + g2[...].astype(F32) + g3[...].astype(F32))
    rows[0:UNITS] = total
    rows[UNITS] = jnp.zeros((24, rank), F32)
    for m, ref in enumerate(slots):
        for other in range(2):
            for s in range(4):
                ref[other, s] = rows[table_ref[BY_CHIP + 8 * m + 4 * other + s]]
    flat = total.reshape(UNITS * 24, rank)
    gram = lax.dot_general(
        flat, flat, (((0,), (0,)), ((), ())), precision=HIGHEST, preferred_element_type=F32
    )
    if joined:
        down = lax.broadcasted_iota(jnp.int32, (rank, rank), 0)
        across = lax.broadcasted_iota(jnp.int32, (rank, rank), 1)
        first = first_ref[...]
        gram_ref[0:rank, :] = jnp.where(down > across, first, gram)
        diagonal = jnp.sum(jnp.where(down == across, first, 0.0), axis=0, keepdims=True)
        gram_ref[rank:, :] = jnp.broadcast_to(diagonal, (8, rank))
    else:
        gram_ref[...] = gram


def gather(table, keep, got, first=None):
    rank = keep.shape[-1]
    joined = first is not None
    vmem = pl.BlockSpec(memory_space=pltpu.VMEM)
    return pl.pallas_call(
        functools.partial(gather_kernel, rank, joined),
        in_specs=[pl.BlockSpec(memory_space=pltpu.SMEM)] + [vmem] * (4 + joined),
        out_specs=[vmem] * 5,
        out_shape=[jax.ShapeDtypeStruct((rank + 8 * joined, rank), F32)]
        + [jax.ShapeDtypeStruct((2, 4, 24, rank), F32)] * 4,
        scratch_shapes=[pltpu.VMEM((UNITS + 1, 24, rank), F32)],
        compiler_params=limit(8),
        cost_estimate=pl.CostEstimate(flops=12 * UNITS * 24 * rank * rank, bytes_accessed=2**20, transcendentals=0),
        name="gather",
    )(table, keep, *got, *([first] if joined else []))


def pack_kernel(s0, s1, s2, s3, out_ref):
    for m, ref in enumerate((s0, s1, s2, s3)):
        out_ref[m] = ref[1]


def pack(slots):
    vmem = pl.BlockSpec(memory_space=pltpu.VMEM)
    return pl.pallas_call(
        pack_kernel,
        in_specs=[vmem] * 4,
        out_specs=vmem,
        out_shape=jax.ShapeDtypeStruct((4,) + slots[0].shape[1:], F32),
        compiler_params=limit(4),
        cost_estimate=pl.CostEstimate(flops=0, bytes_accessed=2**19, transcendentals=0),
        name="pack",
    )(*slots)


def arrange_kernel(rank, table_ref, s0, s1, s2, s3, other_ref, out_ref, units):
    for m, ref in enumerate((s0, s1, s2, s3)):
        units[4 * m : 4 * m + 4] = ref[0]
        units[16 + 4 * m : 20 + 4 * m] = other_ref[m]
    for v in range(0, 27):
        a, b, c = three(units[table_ref[FINAL + v]])
        for i, part in enumerate((a, a, b, a, b, c)):
            out_ref[24 * v : 24 * v + 24, rank * i : rank * (i + 1)] = part.astype(BF16)


def arrange(table, slots, other):
    rank = other.shape[-1]
    vmem = pl.BlockSpec(memory_space=pltpu.VMEM)
    return pl.pallas_call(
        functools.partial(arrange_kernel, rank),
        in_specs=[pl.BlockSpec(memory_space=pltpu.SMEM)] + [vmem] * 5,
        out_specs=vmem,
        out_shape=jax.ShapeDtypeStruct((27 * 24, 6 * rank), BF16),
        scratch_shapes=[pltpu.VMEM((32, 24, rank), F32)],
        compiler_params=limit(6),
        cost_estimate=pl.CostEstimate(flops=0, bytes_accessed=2**21, transcendentals=0),
        name="arrange",
    )(table, *slots, other)


def planes(activations, out_grads, omega):
    layer_count, _, frames, height, widths, channels = activations.shape
    rank = omega.shape[1]
    dp, space = lax.axis_index("dp"), lax.axis_index("space")
    x = space & 1
    me = 8 * dp + space
    core_mask, chip_masks, z_masks = 8, (1, 16, 17), (2, 4, 6)
    table = lax.dynamic_index_in_dim(jnp.asarray(unit_tables()), me, 0, keepdims=False)
    positions = frames * height * widths

    def move(value, mask):
        return swap(value, mask, 32)

    def move_all(values, masks):
        return [move(v, mask) for v, mask in zip(values, masks)]

    acts = activations.reshape(2, positions, channels)
    over = move(acts, core_mask)

    sketched = jnp.dot(out_grads.reshape(-1, channels), omega, preferred_element_type=F32).astype(BF16)
    sketched = sketched.reshape(layer_count, frames, height, widths, rank)
    edge = jnp.where(x == 1, sketched[:, :, height - 1], sketched[:, :, 0])
    pairs = [(i, i + 1) for i in range(1, 7, 2)]
    edge = lax.ppermute(edge, "space", pairs + [(j, i) for i, j in pairs])[:, :, None]
    pieces = pieces_of(table, sketched, edge)

    gram, held = None, []
    for layer in range(2):
        act, *out = turn(table, acts, over, layer, frames)
        got = move_all(out, chip_masks)
        own = [pieces[layer]] + move_all([pieces[layer]] * 3, chip_masks)
        other = [move(piece, core_mask) for piece in own]
        keep, *out = plane(table, act, got, own, other)
        got = move_all(out, z_masks)
        gram, *slots = gather(table, keep, got, gram)
        slots = slots[:1] + move_all(slots[1:], chip_masks)
        other = move(pack(slots), core_mask)
        held.append(arrange(table, slots, other))

    for mask in (core_mask, 4, 2, 1, 16):
        gram = gram + move(gram, mask)
    return finish(gram, *held, math.sqrt(27 * channels))


def solution(mesh):
    def body(activations, out_grads, omega):
        fits = (lax.axis_size("dp"), lax.axis_size("space")) == (4, 8)
        fits = fits and activations.shape == (2, 1, 8, 2, 32, 768) and omega.shape[1] == 128
        return (planes if fits else shards)(activations, out_grads, omega)

    return jax.shard_map(
        body,
        mesh=mesh,
        in_specs=(
            P(None, "dp", None, "space", None, None),
            P(None, "dp", None, "space", None, None),
            P(),
        ),
        out_specs=P(None, ("dp", "space"), None),
        check_vma=False,
    )
```

profile of v0, /device:TPU:0, one launch (start us, length us, event | category | flops | bytes accessed | tf_op | source)
XLA Modules:
  0.0 125.1 jit_solution(11759446982660810728)
XLA Ops:
  0.0 0.5 collective-permute-start
  0.5 0.9 copy-done
  1.4 1.5 %convolution_convert_fusion = bf16[1024,128]{1,0:T(8,128)(2,1)S(1)} fusion(bf16[1024,768]{1,0:T(8,128)(2,1)S(1)} %bitcast.19, bf16[768,128]{1,0:T(8,128)(2,1)} %param.6), kind=kOutput, calls=%fused_computation | convolution fusion | flops 201457664 | bytes 2031616 | tf_op jit(solution)/shard_map/dot_general | solution.py:515
  2.9 0.7 fusion.1
  3.6 0.7 collective-permute-start.4
  4.3 0.7 constant_dynamic-slice_fusion
  5.0 0.6 pieces.1
  5.6 9.9 %collective-permute-start.18 = (bf16[8,3,32,128]{3,2,1,0:T(8,128)(2,1)S(1)}, bf16[8,3,32,128]{3,2,1,0:T(8,128)(2,1)S(1)}, u32[]{:S(2)}, u32[]{:S(2)}) collective-permute-start(bf16[8,3,32,128]{3,2,1,0:T(8,128)(2,1)S(1)} %get-tuple-element.46.refs_4_), channel_id=1, source_target_pairs={{0,1},{1,0},{2,3},{3,2},{4,5},{5,4},{6,7},{7,6},{8,9},{9,8},{10,11... | collective-permute-start | bytes 589832 | tf_op jit(solution)/shard_map/ppermute | solution.py:19
  15.4 1.5 %collective-permute-start.19 = (bf16[8,3,32,128]{3,2,1,0:T(8,128)(2,1)S(1)}, bf16[8,3,32,128]{3,2,1,0:T(8,128)(2,1)S(1)}, u32[]{:S(2)}, u32[]{:S(2)}) collective-permute-start(bf16[8,3,32,128]{3,2,1,0:T(8,128)(2,1)S(1)} %get-tuple-element.46.refs_4_), channel_id=1, source_target_pairs={{0,16},{1,17},{2,18},{3,19},{4,20},{5,21},{6,22},{7,23},{8,24},{9,... | collective-permute-start | bytes 589832 | tf_op jit(solution)/shard_map/ppermute | solution.py:19
  17.0 0.0 collective-permute-start.20
  17.0 4.1 %collective-permute-done.18.refs_5_ = bf16[8,3,32,128]{3,2,1,0:T(8,128)(2,1)S(1)} collective-permute-done((bf16[8,3,32,128]{3,2,1,0:T(8,128)(2,1)S(1)}, bf16[8,3,32,128]{3,2,1,0:T(8,128)(2,1)S(1)}, u32[]{:S(2)}, u32[]{:S(2)}) %collective-permute-start.18) | collective-permute-done | bytes 196640 | tf_op jit(solution)/shard_map/ppermute | solution.py:19
  21.0 1.5 %collective-permute-start.6 = (bf16[8,3,32,128]{3,2,1,0:T(8,128)(2,1)S(1)}, bf16[8,3,32,128]{3,2,1,0:T(8,128)(2,1)S(1)}, u32[]{:S(2)}, u32[]{:S(2)}) collective-permute-start(bf16[8,3,32,128]{3,2,1,0:T(8,128)(2,1)S(1)} %get-tuple-element.37.refs_4_), channel_id=1, source_target_pairs={{0,16},{1,17},{2,18},{3,19},{4,20},{5,21},{6,22},{7,23},{8,24},{9,... | collective-permute-start | bytes 589832 | tf_op jit(solution)/shard_map/ppermute | solution.py:19
  22.6 6.2 %collective-permute-done.19.refs_6_ = bf16[8,3,32,128]{3,2,1,0:T(8,128)(2,1)S(1)} collective-permute-done((bf16[8,3,32,128]{3,2,1,0:T(8,128)(2,1)S(1)}, bf16[8,3,32,128]{3,2,1,0:T(8,128)(2,1)S(1)}, u32[]{:S(2)}, u32[]{:S(2)}) %collective-permute-start.19) | collective-permute-done | bytes 196640 | tf_op jit(solution)/shard_map/ppermute | solution.py:19
  28.7 0.5 collective-permute-start.7
  29.3 2.7 %collective-permute-start.5 = (bf16[8,3,32,128]{3,2,1,0:T(8,128)(2,1)S(1)}, bf16[8,3,32,128]{3,2,1,0:T(8,128)(2,1)S(1)}, u32[]{:S(2)}, u32[]{:S(2)}) collective-permute-start(bf16[8,3,32,128]{3,2,1,0:T(8,128)(2,1)S(1)} %get-tuple-element.37.refs_4_), channel_id=1, source_target_pairs={{0,1},{1,0},{2,3},{3,2},{4,5},{5,4},{6,7},{7,6},{8,9},{9,8},{10,11... | collective-permute-start | bytes 589832 | tf_op jit(solution)/shard_map/ppermute | solution.py:19
  32.0 0.5 collective-permute-start.22
  32.5 0.1 collective-permute-start.23
  32.5 1.5 %turn.3 = (bf16[96,1024]{1,0:T(8,128)(2,1)S(1)}, bf16[96,1024]{1,0:T(8,128)(2,1)S(1)}, bf16[96,1024]{1,0:T(8,128)(2,1)S(1)}, bf16[96,1024]{1,0:T(8,128)(2,1)S(1)}) custom-call(s32[174]{0:T(256)S(1)} %bitcast.27, bf16[2,512,768]{2,1,0:T(8,128)(2,1)S(1)} %bitcast.21, bf16[2,512,768]{2,1,0:T(8,128)(2,1)} %collective-permute-done.got_ref), custom_call_target="tpu_custom_call" | custom-call | bytes 1572864 | tf_op jit(solution)/shard_map/turn/pallas_call | solution.py:299
  34.0 1.3 %collective-permute-done.7.refs_7_ = bf16[8,3,32,128]{3,2,1,0:T(8,128)(2,1)S(1)} collective-permute-done((bf16[8,3,32,128]{3,2,1,0:T(8,128)(2,1)S(1)}, bf16[8,3,32,128]{3,2,1,0:T(8,128)(2,1)S(1)}, u32[]{:S(2)}, u32[]{:S(2)}) %collective-permute-start.7) | collective-permute-done | bytes 196640 | tf_op jit(solution)/shard_map/ppermute | solution.py:19
  35.3 2.4 %collective-permute-done.5.refs_5_ = bf16[8,3,32,128]{3,2,1,0:T(8,128)(2,1)S(1)} collective-permute-done((bf16[8,3,32,128]{3,2,1,0:T(8,128)(2,1)S(1)}, bf16[8,3,32,128]{3,2,1,0:T(8,128)(2,1)S(1)}, u32[]{:S(2)}, u32[]{:S(2)}) %collective-permute-start.5) | collective-permute-done | bytes 196640 | tf_op jit(solution)/shard_map/ppermute | solution.py:19
  37.7 0.6 collective-permute-start.16
  38.3 2.9 %collective-permute-start.17 = (bf16[96,1024]{1,0:T(8,128)(2,1)S(1)}, bf16[96,1024]{1,0:T(8,128)(2,1)S(1)}, u32[]{:S(2)}, u32[]{:S(2)}) collective-permute-start(bf16[96,1024]{1,0:T(8,128)(2,1)S(1)} %get-tuple-element.45), channel_id=1, source_target_pairs={{0,17},{1,16},{2,19},{3,18},{4,21},{5,20},{6,23},{7,22},{8,25},{9,... | collective-permute-start | bytes 589832 | tf_op jit(solution)/shard_map/ppermute | solution.py:19
  41.2 1.5 %turn.2 = (bf16[96,1024]{1,0:T(8,128)(2,1)S(1)}, bf16[96,1024]{1,0:T(8,128)(2,1)S(1)}, bf16[96,1024]{1,0:T(8,128)(2,1)S(1)}, bf16[96,1024]{1,0:T(8,128)(2,1)S(1)}) custom-call(s32[174]{0:T(256)S(1)} %bitcast.28, bf16[2,512,768]{2,1,0:T(8,128)(2,1)S(1)} %bitcast.22, bf16[2,512,768]{2,1,0:T(8,128)(2,1)} %collective-permute-done.got_ref), custom_call_target="tpu_custom_call" | custom-call | bytes 1572864 | tf_op jit(solution)/shard_map/turn/pallas_call | solution.py:299
  42.7 0.1 collective-permute-start.11
  42.8 0.5 collective-permute-start.9
  43.3 2.2 %collective-permute-done.15.refs_1_ = bf16[96,1024]{1,0:T(8,128)(2,1)S(1)} collective-permute-done((bf16[96,1024]{1,0:T(8,128)(2,1)S(1)}, bf16[96,1024]{1,0:T(8,128)(2,1)S(1)}, u32[]{:S(2)}, u32[]{:S(2)}) %collective-permute-start.15) | collective-permute-done | bytes 196640 | tf_op jit(solution)/shard_map/ppermute | solution.py:19
  45.5 4.1 %collective-permute-done.16.refs_2_ = bf16[96,1024]{1,0:T(8,128)(2,1)S(1)} collective-permute-done((bf16[96,1024]{1,0:T(8,128)(2,1)S(1)}, bf16[96,1024]{1,0:T(8,128)(2,1)S(1)}, u32[]{:S(2)}, u32[]{:S(2)}) %collective-permute-start.16) | collective-permute-done | bytes 196640 | tf_op jit(solution)/shard_map/ppermute | solution.py:19
  49.6 2.9 %collective-permute-start.3 = (bf16[96,1024]{1,0:T(8,128)(2,1)S(1)}, bf16[96,1024]{1,0:T(8,128)(2,1)S(1)}, u32[]{:S(2)}, u32[]{:S(2)}) collective-permute-start(bf16[96,1024]{1,0:T(8,128)(2,1)S(1)} %get-tuple-element.36), channel_id=1, source_target_pairs={{0,17},{1,16},{2,19},{3,18},{4,21},{5,20},{6,23},{7,22},{8,25},{9,... | collective-permute-start | bytes 589832 | tf_op jit(solution)/shard_map/ppermute | solution.py:19
  52.4 6.8 %plane.3 = (f32[28,24,128]{2,1,0:T(8,128)S(1)}, bf16[28,24,128]{2,1,0:T(8,128)(2,1)S(1)}, bf16[28,24,128]{2,1,0:T(8,128)(2,1)S(1)}, bf16[28,24,128]{2,1,0:T(8,128)(2,1)S(1)}) custom-call(s32[174]{0:T(256)S(1)} %bitcast.29, bf16[96,1024]{1,0:T(8,128)(2,1)S(1)} %get-tuple-element.42.refs_0_, bf16[96,1024]{1,0:T(8,128)(2,1)S(1)} %collective-permute-done.15.refs_1_, ...), custom_call_target="tpu_custom_call" | custom-call | flops 2717908992 | bytes 6291456 | tf_op jit(solution)/shard_map/plane/pallas_call | solution.py:390
  59.2 1.6 %collective-permute-start.25 = (bf16[28,24,128]{2,1,0:T(8,128)(2,1)S(1)}, bf16[28,24,128]{2,1,0:T(8,128)(2,1)S(1)}, u32[]{:S(2)}, u32[]{:S(2)}) collective-permute-start(bf16[28,24,128]{2,1,0:T(8,128)(2,1)S(1)} %get-tuple-element.48), channel_id=1, source_target_pairs={{0,2},{1,3},{2,0},{3,1},{4,6},{5,7},{6,4},{7,5},{8,10},{9,11},{10,... | collective-permute-start | bytes 516104 | tf_op jit(solution)/shard_map/ppermute | solution.py:19
  60.9 1.7 %collective-permute-start.26 = (bf16[28,24,128]{2,1,0:T(8,128)(2,1)S(1)}, bf16[28,24,128]{2,1,0:T(8,128)(2,1)S(1)}, u32[]{:S(2)}, u32[]{:S(2)}) collective-permute-start(bf16[28,24,128]{2,1,0:T(8,128)(2,1)S(1)} %get-tuple-element.49), channel_id=1, source_target_pairs={{0,4},{1,5},{2,6},{3,7},{4,0},{5,1},{6,2},{7,3},{8,12},{9,13},{10,... | collective-permute-start | bytes 516104 | tf_op jit(solution)/shard_map/ppermute | solution.py:19
  62.6 1.1 collective-permute-start.27
  63.7 6.6 %plane.2 = (f32[28,24,128]{2,1,0:T(8,128)S(1)}, bf16[28,24,128]{2,1,0:T(8,128)(2,1)S(1)}, bf16[28,24,128]{2,1,0:T(8,128)(2,1)S(1)}, bf16[28,24,128]{2,1,0:T(8,128)(2,1)S(1)}) custom-call(s32[174]{0:T(256)S(1)} %bitcast.30, bf16[96,1024]{1,0:T(8,128)(2,1)S(1)} %get-tuple-element.33.refs_0_, bf16[96,1024]{1,0:T(8,128)(2,1)S(1)} %collective-permute-done.1.refs_1_, ...), custom_call_target="tpu_custom_call" | custom-call | flops 2717908992 | bytes 6291456 | tf_op jit(solution)/shard_map/plane/pallas_call | solution.py:390
  70.3 0.7 collective-permute-start.12
  71.0 2.6 %collective-permute-start.13 = (bf16[28,24,128]{2,1,0:T(8,128)(2,1)S(1)}, bf16[28,24,128]{2,1,0:T(8,128)(2,1)S(1)}, u32[]{:S(2)}, u32[]{:S(2)}) collective-permute-start(bf16[28,24,128]{2,1,0:T(8,128)(2,1)S(1)} %get-tuple-element.40), channel_id=1, source_target_pairs={{0,4},{1,5},{2,6},{3,7},{4,0},{5,1},{6,2},{7,3},{8,12},{9,13},{10,... | collective-permute-start | bytes 516104 | tf_op jit(solution)/shard_map/ppermute | solution.py:19
  73.7 1.1 collective-permute-start.14
  74.8 1.2 collective-permute-done.26.refs_2_
  76.0 1.1 gather.2
  77.1 1.4 %collective-permute-done.12.refs_1_ = bf16[28,24,128]{2,1,0:T(8,128)(2,1)S(1)} collective-permute-done((bf16[28,24,128]{2,1,0:T(8,128)(2,1)S(1)}, bf16[28,24,128]{2,1,0:T(8,128)(2,1)S(1)}, u32[]{:S(2)}, u32[]{:S(2)}) %collective-permute-start.12) | collective-permute-done | bytes 172064 | tf_op jit(solution)/shard_map/ppermute | solution.py:19
  78.5 12.1 %collective-permute-done.13.refs_2_ = bf16[28,24,128]{2,1,0:T(8,128)(2,1)S(1)} collective-permute-done((bf16[28,24,128]{2,1,0:T(8,128)(2,1)S(1)}, bf16[28,24,128]{2,1,0:T(8,128)(2,1)S(1)}, u32[]{:S(2)}, u32[]{:S(2)}) %collective-permute-start.13) | collective-permute-done | bytes 172064 | tf_op jit(solution)/shard_map/ppermute | solution.py:19
  90.6 1.1 gather.3
  91.7 0.1 collective-permute-start.28
  91.8 0.5 collective-permute-start.37
  92.3 0.8 collective-permute-done.28
  93.1 3.4 %collective-permute-start.29 = (f32[136,128]{1,0:T(8,128)S(1)}, f32[136,128]{1,0:T(8,128)S(1)}, u32[]{:S(2)}, u32[]{:S(2)}) collective-permute-start(f32[136,128]{1,0:T(8,128)S(1)} %add.24), channel_id=1, source_target_pairs={{0,4},{1,5},{2,6},{3,7},{4,0},{5,1},{6,2},{7,3},{8,12},{9,13},{10,... | collective-permute-start | bytes 208904 | tf_op jit(solution)/shard_map/ppermute | solution.py:19
  96.5 0.3 collective-permute-start.38
  96.8 2.0 %collective-permute-start.39 = (f32[2,4,24,128]{3,2,1,0:T(8,128)S(1)}, f32[2,4,24,128]{3,2,1,0:T(8,128)S(1)}, u32[]{:S(2)}, u32[]{:S(2)}) collective-permute-start(f32[2,4,24,128]{3,2,1,0:T(8,128)S(1)} %get-tuple-element.60), channel_id=1, source_target_pairs={{0,17},{1,16},{2,19},{3,18},{4,21},{5,20},{6,23},{7,22},{8,25},{9,... | collective-permute-start | bytes 294920 | tf_op jit(solution)/shard_map/ppermute | solution.py:19
  98.8 1.2 collective-permute-start.33
  100.0 0.3 collective-permute-start.34
  100.3 0.2 collective-permute-done.29
  100.5 1.8 %collective-permute-start.35 = (f32[2,4,24,128]{3,2,1,0:T(8,128)S(1)}, f32[2,4,24,128]{3,2,1,0:T(8,128)S(1)}, u32[]{:S(2)}, u32[]{:S(2)}) collective-permute-start(f32[2,4,24,128]{3,2,1,0:T(8,128)S(1)} %get-tuple-element.56), channel_id=1, source_target_pairs={{0,17},{1,16},{2,19},{3,18},{4,21},{5,20},{6,23},{7,22},{8,25},{9,... | collective-permute-start | bytes 294920 | tf_op jit(solution)/shard_map/ppermute | solution.py:19
  102.3 2.6 %collective-permute-done.38.s2 = f32[2,4,24,128]{3,2,1,0:T(8,128)S(1)} collective-permute-done((f32[2,4,24,128]{3,2,1,0:T(8,128)S(1)}, f32[2,4,24,128]{3,2,1,0:T(8,128)S(1)}, u32[]{:S(2)}, u32[]{:S(2)}) %collective-permute-start.38) | collective-permute-done | bytes 98336 | tf_op jit(solution)/shard_map/ppermute | solution.py:19
  105.0 0.1 collective-permute-start.40
  105.0 0.4 collective-permute-done.33.s1
  105.4 2.0 %collective-permute-done.34.s2 = f32[2,4,24,128]{3,2,1,0:T(8,128)S(1)} collective-permute-done((f32[2,4,24,128]{3,2,1,0:T(8,128)S(1)}, f32[2,4,24,128]{3,2,1,0:T(8,128)S(1)}, u32[]{:S(2)}, u32[]{:S(2)}) %collective-permute-start.34) | collective-permute-done | bytes 98336 | tf_op jit(solution)/shard_map/ppermute | solution.py:19
  107.4 0.1 collective-permute-start.36
  107.5 1.7 %collective-permute-done.30 = f32[136,128]{1,0:T(8,128)S(1)} collective-permute-done((f32[136,128]{1,0:T(8,128)S(1)}, f32[136,128]{1,0:T(8,128)S(1)}, u32[]{:S(2)}, u32[]{:S(2)}) %collective-permute-start.30) | collective-permute-done | bytes 69664 | tf_op jit(solution)/shard_map/ppermute | solution.py:19
  109.3 0.9 collective-permute-start.31
  110.2 3.5 %collective-permute-done.31 = f32[136,128]{1,0:T(8,128)S(1)} collective-permute-done((f32[136,128]{1,0:T(8,128)S(1)}, f32[136,128]{1,0:T(8,128)S(1)}, u32[]{:S(2)}, u32[]{:S(2)}) %collective-permute-start.31) | collective-permute-done | bytes 69664 | tf_op jit(solution)/shard_map/ppermute | solution.py:19
  113.6 0.1 collective-permute-start.32
  113.7 0.7 arrange.3.second_ref
  114.4 0.7 arrange.2.first_ref
  115.1 2.9 %collective-permute-done.32 = f32[136,128]{1,0:T(8,128)S(1)} collective-permute-done((f32[136,128]{1,0:T(8,128)S(1)}, f32[136,128]{1,0:T(8,128)S(1)}, u32[]{:S(2)}, u32[]{:S(2)}) %collective-permute-start.32) | collective-permute-done | bytes 69664 | tf_op jit(solution)/shard_map/ppermute | solution.py:19
  118.0 7.0 %finish.1 = f32[2,648,128]{2,1,0:T(8,128)} custom-call(f32[136,128]{1,0:T(8,128)S(1)} %add.28.gram_ref, bf16[648,768]{1,0:T(8,128)(2,1)S(1)} %arrange.2.first_ref, bf16[648,768]{1,0:T(8,128)(2,1)S(1)} %arrange.3.second_ref), custom_call_target="tpu_custom_call" | custom-call | flops 2147483648 | bytes 4194304 | tf_op jit(solution)/shard_map/finish/pallas_call | solution.py:167
  (42 shorter events, 0.2 us)
Async XLA Ops:
  0.0 1.4 %copy-start = (bf16[2,1,8,2,32,768]{5,4,3,2,1,0:T(8,128)(2,1)S(1)}, bf16[2,1,8,2,32,768]{5,4,3,2,1,0:T(8,128)(2,1)}, u32[]{:S(2)}) copy-start(bf16[2,1,8,2,32,768]{5,4,3,2,1,0:T(8,128)(2,1)} %param.5) | copy-start | bytes 4718596
  0.0 32.5 %copy-start.1 = (bf16[2,1,8,2,32,768]{5,4,3,2,1,0:T(8,128)(2,1)S(1)}, bf16[2,1,8,2,32,768]{5,4,3,2,1,0:T(8,128)(2,1)}, u32[]{:S(2)}) copy-start(bf16[2,1,8,2,32,768]{5,4,3,2,1,0:T(8,128)(2,1)} %param.4) | copy-start | bytes 4718596
  0.0 32.5 %collective-permute-start = (bf16[2,512,768]{2,1,0:T(8,128)(2,1)}, bf16[2,512,768]{2,1,0:T(8,128)(2,1)}, u32[]{:S(2)}, u32[]{:S(2)}) collective-permute-start(bf16[2,512,768]{2,1,0:T(8,128)(2,1)} %bitcast.20), channel_id=1, source_target_pairs={{0,8},{1,9},{2,10},{3,11},{4,12},{5,13},{6,14},{7,15},{8,0},{9,1},... | collective-permute-start | bytes 4718600 | tf_op jit(solution)/shard_map/ppermute | solution.py:19
  3.6 1.4 %collective-permute-start.4 = (bf16[2,8,32,128]{3,2,1,0:T(8,128)(2,1)}, bf16[2,8,32,128]{3,2,1,0:T(8,128)(2,1)S(1)}, u32[]{:S(2)}, u32[]{:S(2)}) collective-permute-start(bf16[2,8,32,128]{3,2,1,0:T(8,128)(2,1)} %fusion.1), channel_id=1, source_target_pairs={{1,2},{3,4},{5,6},{2,1},{4,3},{6,5},{9,10},{11,12},{13,14},{10,9},... | collective-permute-start | bytes 393224 | tf_op jit(solution)/shard_map/ppermute | solution.py:519
  5.6 15.5 %collective-permute-start.18 = (bf16[8,3,32,128]{3,2,1,0:T(8,128)(2,1)S(1)}, bf16[8,3,32,128]{3,2,1,0:T(8,128)(2,1)S(1)}, u32[]{:S(2)}, u32[]{:S(2)}) collective-permute-start(bf16[8,3,32,128]{3,2,1,0:T(8,128)(2,1)S(1)} %get-tuple-element.46.refs_4_), channel_id=1, source_target_pairs={{0,1},{1,0},{2,3},{3,2},{4,5},{5,4},{6,7},{7,6},{8,9},{9,8},{10,11... | collective-permute-start | bytes 589832 | tf_op jit(solution)/shard_map/ppermute | solution.py:19
  15.4 13.3 %collective-permute-start.19 = (bf16[8,3,32,128]{3,2,1,0:T(8,128)(2,1)S(1)}, bf16[8,3,32,128]{3,2,1,0:T(8,128)(2,1)S(1)}, u32[]{:S(2)}, u32[]{:S(2)}) collective-permute-start(bf16[8,3,32,128]{3,2,1,0:T(8,128)(2,1)S(1)} %get-tuple-element.46.refs_4_), channel_id=1, source_target_pairs={{0,16},{1,17},{2,18},{3,19},{4,20},{5,21},{6,22},{7,23},{8,24},{9,... | collective-permute-start | bytes 589832 | tf_op jit(solution)/shard_map/ppermute | solution.py:19
  17.0 12.3 %collective-permute-start.20 = (bf16[8,3,32,128]{3,2,1,0:T(8,128)(2,1)S(1)}, bf16[8,3,32,128]{3,2,1,0:T(8,128)(2,1)S(1)}, u32[]{:S(2)}, u32[]{:S(2)}) collective-permute-start(bf16[8,3,32,128]{3,2,1,0:T(8,128)(2,1)S(1)} %get-tuple-element.46.refs_4_), channel_id=1, source_target_pairs={{0,17},{1,16},{2,19},{3,18},{4,21},{5,20},{6,23},{7,22},{8,25},{9,... | collective-permute-start | bytes 589832 | tf_op jit(solution)/shard_map/ppermute | solution.py:19
  17.0 15.0 %collective-permute-start.21 = (bf16[8,3,32,128]{3,2,1,0:T(8,128)(2,1)S(1)}, bf16[8,3,32,128]{3,2,1,0:T(8,128)(2,1)S(1)}, u32[]{:S(2)}, u32[]{:S(2)}) collective-permute-start(bf16[8,3,32,128]{3,2,1,0:T(8,128)(2,1)S(1)} %get-tuple-element.46.refs_4_), channel_id=1, source_target_pairs={{0,8},{1,9},{2,10},{3,11},{4,12},{5,13},{6,14},{7,15},{8,0},{9,1},... | collective-permute-start | bytes 589832 | tf_op jit(solution)/shard_map/ppermute | solution.py:19
  21.0 10.9 %collective-permute-start.6 = (bf16[8,3,32,128]{3,2,1,0:T(8,128)(2,1)S(1)}, bf16[8,3,32,128]{3,2,1,0:T(8,128)(2,1)S(1)}, u32[]{:S(2)}, u32[]{:S(2)}) collective-permute-start(bf16[8,3,32,128]{3,2,1,0:T(8,128)(2,1)S(1)} %get-tuple-element.37.refs_4_), channel_id=1, source_target_pairs={{0,16},{1,17},{2,18},{3,19},{4,20},{5,21},{6,22},{7,23},{8,24},{9,... | collective-permute-start | bytes 589832 | tf_op jit(solution)/shard_map/ppermute | solution.py:19
  28.7 6.6 %collective-permute-start.7 = (bf16[8,3,32,128]{3,2,1,0:T(8,128)(2,1)S(1)}, bf16[8,3,32,128]{3,2,1,0:T(8,128)(2,1)S(1)}, u32[]{:S(2)}, u32[]{:S(2)}) collective-permute-start(bf16[8,3,32,128]{3,2,1,0:T(8,128)(2,1)S(1)} %get-tuple-element.37.refs_4_), channel_id=1, source_target_pairs={{0,17},{1,16},{2,19},{3,18},{4,21},{5,20},{6,23},{7,22},{8,25},{9,... | collective-permute-start | bytes 589832 | tf_op jit(solution)/shard_map/ppermute | solution.py:19
  29.3 8.4 %collective-permute-start.5 = (bf16[8,3,32,128]{3,2,1,0:T(8,128)(2,1)S(1)}, bf16[8,3,32,128]{3,2,1,0:T(8,128)(2,1)S(1)}, u32[]{:S(2)}, u32[]{:S(2)}) collective-permute-start(bf16[8,3,32,128]{3,2,1,0:T(8,128)(2,1)S(1)} %get-tuple-element.37.refs_4_), channel_id=1, source_target_pairs={{0,1},{1,0},{2,3},{3,2},{4,5},{5,4},{6,7},{7,6},{8,9},{9,8},{10,11... | collective-permute-start | bytes 589832 | tf_op jit(solution)/shard_map/ppermute | solution.py:19
  31.9 5.7 %collective-permute-start.8 = (bf16[8,3,32,128]{3,2,1,0:T(8,128)(2,1)S(1)}, bf16[8,3,32,128]{3,2,1,0:T(8,128)(2,1)S(1)}, u32[]{:S(2)}, u32[]{:S(2)}) collective-permute-start(bf16[8,3,32,128]{3,2,1,0:T(8,128)(2,1)S(1)} %get-tuple-element.37.refs_4_), channel_id=1, source_target_pairs={{0,8},{1,9},{2,10},{3,11},{4,12},{5,13},{6,14},{7,15},{8,0},{9,1},... | collective-permute-start | bytes 589832 | tf_op jit(solution)/shard_map/ppermute | solution.py:19
  32.0 5.8 %collective-permute-start.22 = (bf16[8,3,32,128]{3,2,1,0:T(8,128)(2,1)S(1)}, bf16[8,3,32,128]{3,2,1,0:T(8,128)(2,1)S(1)}, u32[]{:S(2)}, u32[]{:S(2)}) collective-permute-start(bf16[8,3,32,128]{3,2,1,0:T(8,128)(2,1)S(1)} %collective-permute-done.18.refs_5_), channel_id=1, source_target_pairs={{0,8},{1,9},{2,10},{3,11},{4,12},{5,13},{6,14},{7,15},{8,0},{9,1},... | collective-permute-start | bytes 589832 | tf_op jit(solution)/shard_map/ppermute | solution.py:19
  32.5 5.8 %collective-permute-start.23 = (bf16[8,3,32,128]{3,2,1,0:T(8,128)(2,1)S(1)}, bf16[8,3,32,128]{3,2,1,0:T(8,128)(2,1)S(1)}, u32[]{:S(2)}, u32[]{:S(2)}) collective-permute-start(bf16[8,3,32,128]{3,2,1,0:T(8,128)(2,1)S(1)} %collective-permute-done.19.refs_6_), channel_id=1, source_target_pairs={{0,8},{1,9},{2,10},{3,11},{4,12},{5,13},{6,14},{7,15},{8,0},{9,1},... | collective-permute-start | bytes 589832 | tf_op jit(solution)/shard_map/ppermute | solution.py:19
  35.3 7.4 %collective-permute-start.24 = (bf16[8,3,32,128]{3,2,1,0:T(8,128)(2,1)S(1)}, bf16[8,3,32,128]{3,2,1,0:T(8,128)(2,1)S(1)}, u32[]{:S(2)}, u32[]{:S(2)}) collective-permute-start(bf16[8,3,32,128]{3,2,1,0:T(8,128)(2,1)S(1)} %collective-permute-done.20.refs_7_), channel_id=1, source_target_pairs={{0,8},{1,9},{2,10},{3,11},{4,12},{5,13},{6,14},{7,15},{8,0},{9,1},... | collective-permute-start | bytes 589832 | tf_op jit(solution)/shard_map/ppermute | solution.py:19
  37.7 5.1 %collective-permute-start.10 = (bf16[8,3,32,128]{3,2,1,0:T(8,128)(2,1)S(1)}, bf16[8,3,32,128]{3,2,1,0:T(8,128)(2,1)S(1)}, u32[]{:S(2)}, u32[]{:S(2)}) collective-permute-start(bf16[8,3,32,128]{3,2,1,0:T(8,128)(2,1)S(1)} %collective-permute-done.6.refs_6_), channel_id=1, source_target_pairs={{0,8},{1,9},{2,10},{3,11},{4,12},{5,13},{6,14},{7,15},{8,0},{9,1},... | collective-permute-start | bytes 589832 | tf_op jit(solution)/shard_map/ppermute | solution.py:19
  37.7 7.8 %collective-permute-start.15 = (bf16[96,1024]{1,0:T(8,128)(2,1)S(1)}, bf16[96,1024]{1,0:T(8,128)(2,1)S(1)}, u32[]{:S(2)}, u32[]{:S(2)}) collective-permute-start(bf16[96,1024]{1,0:T(8,128)(2,1)S(1)} %get-tuple-element.43), channel_id=1, source_target_pairs={{0,1},{1,0},{2,3},{3,2},{4,5},{5,4},{6,7},{7,6},{8,9},{9,8},{10,11... | collective-permute-start | bytes 589832 | tf_op jit(solution)/shard_map/ppermute | solution.py:19
  37.7 11.8 %collective-permute-start.16 = (bf16[96,1024]{1,0:T(8,128)(2,1)S(1)}, bf16[96,1024]{1,0:T(8,128)(2,1)S(1)}, u32[]{:S(2)}, u32[]{:S(2)}) collective-permute-start(bf16[96,1024]{1,0:T(8,128)(2,1)S(1)} %get-tuple-element.44), channel_id=1, source_target_pairs={{0,16},{1,17},{2,18},{3,19},{4,20},{5,21},{6,22},{7,23},{8,24},{9,... | collective-permute-start | bytes 589832 | tf_op jit(solution)/shard_map/ppermute | solution.py:19
  38.3 11.3 %collective-permute-start.17 = (bf16[96,1024]{1,0:T(8,128)(2,1)S(1)}, bf16[96,1024]{1,0:T(8,128)(2,1)S(1)}, u32[]{:S(2)}, u32[]{:S(2)}) collective-permute-start(bf16[96,1024]{1,0:T(8,128)(2,1)S(1)} %get-tuple-element.45), channel_id=1, source_target_pairs={{0,17},{1,16},{2,19},{3,18},{4,21},{5,20},{6,23},{7,22},{8,25},{9,... | collective-permute-start | bytes 589832 | tf_op jit(solution)/shard_map/ppermute | solution.py:19
  42.7 16.5 %collective-permute-start.11 = (bf16[8,3,32,128]{3,2,1,0:T(8,128)(2,1)S(1)}, bf16[8,3,32,128]{3,2,1,0:T(8,128)(2,1)S(1)}, u32[]{:S(2)}, u32[]{:S(2)}) collective-permute-start(bf16[8,3,32,128]{3,2,1,0:T(8,128)(2,1)S(1)} %collective-permute-done.7.refs_7_), channel_id=1, source_target_pairs={{0,8},{1,9},{2,10},{3,11},{4,12},{5,13},{6,14},{7,15},{8,0},{9,1},... | collective-permute-start | bytes 589832 | tf_op jit(solution)/shard_map/ppermute | solution.py:19
  42.8 18.1 %collective-permute-start.9 = (bf16[8,3,32,128]{3,2,1,0:T(8,128)(2,1)S(1)}, bf16[8,3,32,128]{3,2,1,0:T(8,128)(2,1)S(1)}, u32[]{:S(2)}, u32[]{:S(2)}) collective-permute-start(bf16[8,3,32,128]{3,2,1,0:T(8,128)(2,1)S(1)} %collective-permute-done.5.refs_5_), channel_id=1, source_target_pairs={{0,8},{1,9},{2,10},{3,11},{4,12},{5,13},{6,14},{7,15},{8,0},{9,1},... | collective-permute-start | bytes 589832 | tf_op jit(solution)/shard_map/ppermute | solution.py:19
  45.5 17.1 %collective-permute-start.1 = (bf16[96,1024]{1,0:T(8,128)(2,1)S(1)}, bf16[96,1024]{1,0:T(8,128)(2,1)S(1)}, u32[]{:S(2)}, u32[]{:S(2)}) collective-permute-start(bf16[96,1024]{1,0:T(8,128)(2,1)S(1)} %get-tuple-element.34), channel_id=1, source_target_pairs={{0,1},{1,0},{2,3},{3,2},{4,5},{5,4},{6,7},{7,6},{8,9},{9,8},{10,11... | collective-permute-start | bytes 589832 | tf_op jit(solution)/shard_map/ppermute | solution.py:19
  49.6 14.1 %collective-permute-start.2 = (bf16[96,1024]{1,0:T(8,128)(2,1)S(1)}, bf16[96,1024]{1,0:T(8,128)(2,1)S(1)}, u32[]{:S(2)}, u32[]{:S(2)}) collective-permute-start(bf16[96,1024]{1,0:T(8,128)(2,1)S(1)} %get-tuple-element.35), channel_id=1, source_target_pairs={{0,16},{1,17},{2,18},{3,19},{4,20},{5,21},{6,22},{7,23},{8,24},{9,... | collective-permute-start | bytes 589832 | tf_op jit(solution)/shard_map/ppermute | solution.py:19
  49.6 14.1 %collective-permute-start.3 = (bf16[96,1024]{1,0:T(8,128)(2,1)S(1)}, bf16[96,1024]{1,0:T(8,128)(2,1)S(1)}, u32[]{:S(2)}, u32[]{:S(2)}) collective-permute-start(bf16[96,1024]{1,0:T(8,128)(2,1)S(1)} %get-tuple-element.36), channel_id=1, source_target_pairs={{0,17},{1,16},{2,19},{3,18},{4,21},{5,20},{6,23},{7,22},{8,25},{9,... | collective-permute-start | bytes 589832 | tf_op jit(solution)/shard_map/ppermute | solution.py:19
  59.2 14.4 %collective-permute-start.25 = (bf16[28,24,128]{2,1,0:T(8,128)(2,1)S(1)}, bf16[28,24,128]{2,1,0:T(8,128)(2,1)S(1)}, u32[]{:S(2)}, u32[]{:S(2)}) collective-permute-start(bf16[28,24,128]{2,1,0:T(8,128)(2,1)S(1)} %get-tuple-element.48), channel_id=1, source_target_pairs={{0,2},{1,3},{2,0},{3,1},{4,6},{5,7},{6,4},{7,5},{8,10},{9,11},{10,... | collective-permute-start | bytes 516104 | tf_op jit(solution)/shard_map/ppermute | solution.py:19
  60.9 15.1 %collective-permute-start.26 = (bf16[28,24,128]{2,1,0:T(8,128)(2,1)S(1)}, bf16[28,24,128]{2,1,0:T(8,128)(2,1)S(1)}, u32[]{:S(2)}, u32[]{:S(2)}) collective-permute-start(bf16[28,24,128]{2,1,0:T(8,128)(2,1)S(1)} %get-tuple-element.49), channel_id=1, source_target_pairs={{0,4},{1,5},{2,6},{3,7},{4,0},{5,1},{6,2},{7,3},{8,12},{9,13},{10,... | collective-permute-start | bytes 516104 | tf_op jit(solution)/shard_map/ppermute | solution.py:19
  62.6 13.4 %collective-permute-start.27 = (bf16[28,24,128]{2,1,0:T(8,128)(2,1)S(1)}, bf16[28,24,128]{2,1,0:T(8,128)(2,1)S(1)}, u32[]{:S(2)}, u32[]{:S(2)}) collective-permute-start(bf16[28,24,128]{2,1,0:T(8,128)(2,1)S(1)} %get-tuple-element.50), channel_id=1, source_target_pairs={{0,6},{1,7},{2,4},{3,5},{4,2},{5,3},{6,0},{7,1},{8,14},{9,15},{10,... | collective-permute-start | bytes 516104 | tf_op jit(solution)/shard_map/ppermute | solution.py:19
  70.3 8.2 %collective-permute-start.12 = (bf16[28,24,128]{2,1,0:T(8,128)(2,1)S(1)}, bf16[28,24,128]{2,1,0:T(8,128)(2,1)S(1)}, u32[]{:S(2)}, u32[]{:S(2)}) collective-permute-start(bf16[28,24,128]{2,1,0:T(8,128)(2,1)S(1)} %get-tuple-element.39), channel_id=1, source_target_pairs={{0,2},{1,3},{2,0},{3,1},{4,6},{5,7},{6,4},{7,5},{8,10},{9,11},{10,... | collective-permute-start | bytes 516104 | tf_op jit(solution)/shard_map/ppermute | solution.py:19
  71.0 19.6 %collective-permute-start.13 = (bf16[28,24,128]{2,1,0:T(8,128)(2,1)S(1)}, bf16[28,24,128]{2,1,0:T(8,128)(2,1)S(1)}, u32[]{:S(2)}, u32[]{:S(2)}) collective-permute-start(bf16[28,24,128]{2,1,0:T(8,128)(2,1)S(1)} %get-tuple-element.40), channel_id=1, source_target_pairs={{0,4},{1,5},{2,6},{3,7},{4,0},{5,1},{6,2},{7,3},{8,12},{9,13},{10,... | collective-permute-start | bytes 516104 | tf_op jit(solution)/shard_map/ppermute | solution.py:19
  73.7 16.9 %collective-permute-start.14 = (bf16[28,24,128]{2,1,0:T(8,128)(2,1)S(1)}, bf16[28,24,128]{2,1,0:T(8,128)(2,1)S(1)}, u32[]{:S(2)}, u32[]{:S(2)}) collective-permute-start(bf16[28,24,128]{2,1,0:T(8,128)(2,1)S(1)} %get-tuple-element.41), channel_id=1, source_target_pairs={{0,6},{1,7},{2,4},{3,5},{4,2},{5,3},{6,0},{7,1},{8,14},{9,15},{10,... | collective-permute-start | bytes 516104 | tf_op jit(solution)/shard_map/ppermute | solution.py:19
  91.7 1.3 %collective-permute-start.28 = (f32[136,128]{1,0:T(8,128)S(1)}, f32[136,128]{1,0:T(8,128)S(1)}, u32[]{:S(2)}, u32[]{:S(2)}) collective-permute-start(f32[136,128]{1,0:T(8,128)S(1)} %get-tuple-element.52), channel_id=1, source_target_pairs={{0,8},{1,9},{2,10},{3,11},{4,12},{5,13},{6,14},{7,15},{8,0},{9,1},... | collective-permute-start | bytes 208904 | tf_op jit(solution)/shard_map/ppermute | solution.py:19
  91.8 8.2 %collective-permute-start.37 = (f32[2,4,24,128]{3,2,1,0:T(8,128)S(1)}, f32[2,4,24,128]{3,2,1,0:T(8,128)S(1)}, u32[]{:S(2)}, u32[]{:S(2)}) collective-permute-start(f32[2,4,24,128]{3,2,1,0:T(8,128)S(1)} %get-tuple-element.58), channel_id=1, source_target_pairs={{0,1},{1,0},{2,3},{3,2},{4,5},{5,4},{6,7},{7,6},{8,9},{9,8},{10,11... | collective-permute-start | bytes 294920 | tf_op jit(solution)/shard_map/ppermute | solution.py:19
  93.1 7.4 %collective-permute-start.29 = (f32[136,128]{1,0:T(8,128)S(1)}, f32[136,128]{1,0:T(8,128)S(1)}, u32[]{:S(2)}, u32[]{:S(2)}) collective-permute-start(f32[136,128]{1,0:T(8,128)S(1)} %add.24), channel_id=1, source_target_pairs={{0,4},{1,5},{2,6},{3,7},{4,0},{5,1},{6,2},{7,3},{8,12},{9,13},{10,... | collective-permute-start | bytes 208904 | tf_op jit(solution)/shard_map/ppermute | solution.py:19
  96.5 8.4 %collective-permute-start.38 = (f32[2,4,24,128]{3,2,1,0:T(8,128)S(1)}, f32[2,4,24,128]{3,2,1,0:T(8,128)S(1)}, u32[]{:S(2)}, u32[]{:S(2)}) collective-permute-start(f32[2,4,24,128]{3,2,1,0:T(8,128)S(1)} %get-tuple-element.59), channel_id=1, source_target_pairs={{0,16},{1,17},{2,18},{3,19},{4,20},{5,21},{6,22},{7,23},{8,24},{9,... | collective-permute-start | bytes 294920 | tf_op jit(solution)/shard_map/ppermute | solution.py:19
  96.8 8.2 %collective-permute-start.39 = (f32[2,4,24,128]{3,2,1,0:T(8,128)S(1)}, f32[2,4,24,128]{3,2,1,0:T(8,128)S(1)}, u32[]{:S(2)}, u32[]{:S(2)}) collective-permute-start(f32[2,4,24,128]{3,2,1,0:T(8,128)S(1)} %get-tuple-element.60), channel_id=1, source_target_pairs={{0,17},{1,16},{2,19},{3,18},{4,21},{5,20},{6,23},{7,22},{8,25},{9,... | collective-permute-start | bytes 294920 | tf_op jit(solution)/shard_map/ppermute | solution.py:19
  98.8 6.6 %collective-permute-start.33 = (f32[2,4,24,128]{3,2,1,0:T(8,128)S(1)}, f32[2,4,24,128]{3,2,1,0:T(8,128)S(1)}, u32[]{:S(2)}, u32[]{:S(2)}) collective-permute-start(f32[2,4,24,128]{3,2,1,0:T(8,128)S(1)} %get-tuple-element.54), channel_id=1, source_target_pairs={{0,1},{1,0},{2,3},{3,2},{4,5},{5,4},{6,7},{7,6},{8,9},{9,8},{10,11... | collective-permute-start | bytes 294920 | tf_op jit(solution)/shard_map/ppermute | solution.py:19
  100.0 7.4 %collective-permute-start.34 = (f32[2,4,24,128]{3,2,1,0:T(8,128)S(1)}, f32[2,4,24,128]{3,2,1,0:T(8,128)S(1)}, u32[]{:S(2)}, u32[]{:S(2)}) collective-permute-start(f32[2,4,24,128]{3,2,1,0:T(8,128)S(1)} %get-tuple-element.55), channel_id=1, source_target_pairs={{0,16},{1,17},{2,18},{3,19},{4,20},{5,21},{6,22},{7,23},{8,24},{9,... | collective-permute-start | bytes 294920 | tf_op jit(solution)/shard_map/ppermute | solution.py:19
  100.5 6.9 %collective-permute-start.35 = (f32[2,4,24,128]{3,2,1,0:T(8,128)S(1)}, f32[2,4,24,128]{3,2,1,0:T(8,128)S(1)}, u32[]{:S(2)}, u32[]{:S(2)}) collective-permute-start(f32[2,4,24,128]{3,2,1,0:T(8,128)S(1)} %get-tuple-element.56), channel_id=1, source_target_pairs={{0,17},{1,16},{2,19},{3,18},{4,21},{5,20},{6,23},{7,22},{8,25},{9,... | collective-permute-start | bytes 294920 | tf_op jit(solution)/shard_map/ppermute | solution.py:19
  104.9 4.3 %collective-permute-start.30 = (f32[136,128]{1,0:T(8,128)S(1)}, f32[136,128]{1,0:T(8,128)S(1)}, u32[]{:S(2)}, u32[]{:S(2)}) collective-permute-start(f32[136,128]{1,0:T(8,128)S(1)} %add.25), channel_id=1, source_target_pairs={{0,2},{1,3},{2,0},{3,1},{4,6},{5,7},{6,4},{7,5},{8,10},{9,11},{10,... | collective-permute-start | bytes 208904 | tf_op jit(solution)/shard_map/ppermute | solution.py:19
  105.0 8.8 %collective-permute-start.40 = (f32[4,4,24,128]{3,2,1,0:T(8,128)S(1)}, f32[4,4,24,128]{3,2,1,0:T(8,128)S(1)}, u32[]{:S(2)}, u32[]{:S(2)}) collective-permute-start(f32[4,4,24,128]{3,2,1,0:T(8,128)S(1)} %pack.3), channel_id=1, source_target_pairs={{0,8},{1,9},{2,10},{3,11},{4,12},{5,13},{6,14},{7,15},{8,0},{9,1},... | collective-permute-start | bytes 589832 | tf_op jit(solution)/shard_map/ppermute | solution.py:19
  107.4 7.0 %collective-permute-start.36 = (f32[4,4,24,128]{3,2,1,0:T(8,128)S(1)}, f32[4,4,24,128]{3,2,1,0:T(8,128)S(1)}, u32[]{:S(2)}, u32[]{:S(2)}) collective-permute-start(f32[4,4,24,128]{3,2,1,0:T(8,128)S(1)} %pack.2), channel_id=1, source_target_pairs={{0,8},{1,9},{2,10},{3,11},{4,12},{5,13},{6,14},{7,15},{8,0},{9,1},... | collective-permute-start | bytes 589832 | tf_op jit(solution)/shard_map/ppermute | solution.py:19
  109.3 4.4 %collective-permute-start.31 = (f32[136,128]{1,0:T(8,128)S(1)}, f32[136,128]{1,0:T(8,128)S(1)}, u32[]{:S(2)}, u32[]{:S(2)}) collective-permute-start(f32[136,128]{1,0:T(8,128)S(1)} %add.26), channel_id=1, source_target_pairs={{0,1},{1,0},{2,3},{3,2},{4,5},{5,4},{6,7},{7,6},{8,9},{9,8},{10,11... | collective-permute-start | bytes 208904 | tf_op jit(solution)/shard_map/ppermute | solution.py:19
  113.6 4.4 %collective-permute-start.32 = (f32[136,128]{1,0:T(8,128)S(1)}, f32[136,128]{1,0:T(8,128)S(1)}, u32[]{:S(2)}, u32[]{:S(2)}) collective-permute-start(f32[136,128]{1,0:T(8,128)S(1)} %add.27), channel_id=1, source_target_pairs={{0,16},{1,17},{2,18},{3,19},{4,20},{5,21},{6,22},{7,23},{8,24},{9,... | collective-permute-start | bytes 208904 | tf_op jit(solution)/shard_map/ppermute | solution.py:19
where the time goes:
time: 125 us
  waiting for transfers between devices  49 us (39%)
  starting transfers between devices  44.4 us (36%)
  Pallas kernels  27.6 us (22%)
  local copies, waits for them, and re-layouts  1.63 us (1%)
  matrix products  1.5 us (1%)
    ppermute x40, waiting for transfers between devices, swap(): return lax.ppermute(value, AXES, [(d, d ^ mask) for d in range(total)])  49 us
    ppermute x40, starting transfers between devices, swap(): return lax.ppermute(value, AXES, [(d, d ^ mask) for d in range(total)])  43.7 us
    pallas_call x2, Pallas kernels, plane(): pl.pallas_call(functools.partial(plane_kernel, frames, widths, rank), in_...  13.4 us
    pallas_call x1, Pallas kernels, finish(): pl.pallas_call(functools.partial(finish_kernel, size, scale), out_shape=j...  7.04 us
    pallas_call x2, Pallas kernels, turn(): pl.pallas_call(functools.partial(turn_kernel, frames, positions // frames...  2.94 us
  transfers between devices with their start and end apart: 41, of which 17 were waited for; matrix products, arithmetic and copies ran while one was open for 2% of the time, Pallas kernels for 15%

commit v1 on v0

--- a/solution.py
+++ b/solution.py
@@ -142,12 +142,15 @@
     )(gram)
 
 
-def finish_kernel(size, scale, gram_ref, first_ref, second_ref, out_ref, one, two, high, middle, low):
+def finish_kernel(size, scale, table_ref, mine_ref, theirs_ref, first_ref, second_ref, out_ref, one, two, high, middle, low):
     down = lax.broadcasted_iota(jnp.int32, (size, size), 0)
     across = lax.broadcasted_iota(jnp.int32, (size, size), 1)
-    packed = gram_ref[0:size, :]
+    core, half = table_ref[PLACE], size // 2 + 8
+    top = jnp.where(core == 0, mine_ref[...], theirs_ref[...])
+    bottom = jnp.where(core == 0, theirs_ref[...], mine_ref[...])
+    packed = jnp.concatenate([top, bottom[: size - half]], axis=0)
     under = jnp.where(down > across, packed, 0.0)
-    first = under + under.T + jnp.where(down == across, gram_ref[size : size + 1, :], 0.0)
+    first = under + under.T + jnp.where(down == across, bottom[size - half : size - half + 1, :], 0.0)
     second = jnp.where(down <= across, packed, jnp.where(down < across, packed, 0.0).T)
 
     def put(i, start, value):
@@ -162,16 +165,19 @@
         out_ref[i] = made * scale
 
 
-def finish(packed, first, second, scale):
-    size = packed.shape[-1]
+def finish(table, mine, theirs, first, second, scale):
+    size = mine.shape[-1]
+    vmem = pl.BlockSpec(memory_space=pltpu.VMEM)
     return pl.pallas_call(
         functools.partial(finish_kernel, size, scale),
+        in_specs=[pl.BlockSpec(memory_space=pltpu.SMEM)] + [vmem] * 4,
+        out_specs=vmem,
         out_shape=jax.ShapeDtypeStruct((2, first.shape[0], size), F32),
         scratch_shapes=[pltpu.VMEM((size, 2 * size), F32)] * 2 + [pltpu.VMEM((2, size, size), F32)] * 3,
         compiler_params=pltpu.CompilerParams(vmem_limit_bytes=8 * 2**20),
         cost_estimate=pl.CostEstimate(flops=2**31, bytes_accessed=2**22, transcendentals=0),
         name="finish",
-    )(packed, first, second)
+    )(table, mine, theirs, first, second)
 
 
 def pick(value, index, axis):
@@ -410,7 +416,7 @@
 def gather_kernel(rank, joined, table_ref, *refs):
     (keep_ref, g1, g2, g3), refs = refs[:4], refs[4:]
     first_ref, refs = (refs[0], refs[1:]) if joined else (None, refs)
-    gram_ref, slots, rows = refs[0], refs[1:5], refs[5]
+    grams, slots, rows = refs[: 1 + joined], refs[1 + joined : 5 + joined], refs[5 + joined]
     total = keep_ref[...] + (g1[...].astype(F32) + g2[...].astype(F32) + g3[...].astype(F32))
     rows[0:UNITS] = total
     rows[UNITS] = jnp.zeros((24, rank), F32)
@@ -426,24 +432,31 @@
         down = lax.broadcasted_iota(jnp.int32, (rank, rank), 0)
         across = lax.broadcasted_iota(jnp.int32, (rank, rank), 1)
         first = first_ref[...]
-        gram_ref[0:rank, :] = jnp.where(down > across, first, gram)
         diagonal = jnp.sum(jnp.where(down == across, first, 0.0), axis=0, keepdims=True)
-        gram_ref[rank:, :] = jnp.broadcast_to(diagonal, (8, rank))
+        both, half = refs[-1], rank // 2 + 8
+        packed = jnp.where(down > across, first, gram)
+        both[0] = packed[:half]
+        both[1, : rank - half] = packed[half:]
+        both[1, rank - half :] = jnp.broadcast_to(diagonal, (2 * half - rank, rank))
+        core = table_ref[PLACE]
+        grams[0][...] = both[core]
+        grams[1][...] = both[1 - core]
     else:
-        gram_ref[...] = gram
+        grams[0][...] = gram
 
 
 def gather(table, keep, got, first=None):
     rank = keep.shape[-1]
     joined = first is not None
+    gram = (rank // 2 + 8, rank) if joined else (rank, rank)
     vmem = pl.BlockSpec(memory_space=pltpu.VMEM)
     return pl.pallas_call(
         functools.partial(gather_kernel, rank, joined),
         in_specs=[pl.BlockSpec(memory_space=pltpu.SMEM)] + [vmem] * (4 + joined),
-        out_specs=[vmem] * 5,
-        out_shape=[jax.ShapeDtypeStruct((rank + 8 * joined, rank), F32)]
+        out_specs=[vmem] * (5 + joined),
+        out_shape=[jax.ShapeDtypeStruct(gram, F32)] * (1 + joined)
         + [jax.ShapeDtypeStruct((2, 4, 24, rank), F32)] * 4,
-        scratch_shapes=[pltpu.VMEM((UNITS + 1, 24, rank), F32)],
+        scratch_shapes=[pltpu.VMEM((UNITS + 1, 24, rank), F32)] + [pltpu.VMEM((2,) + gram, F32)] * joined,
         compiler_params=limit(8),
         cost_estimate=pl.CostEstimate(flops=12 * UNITS * 24 * rank * rank, bytes_accessed=2**20, transcendentals=0),
         name="gather",
@@ -527,14 +540,18 @@
         other = [move(piece, core_mask) for piece in own]
         keep, *out = plane(table, act, got, own, other)
         got = move_all(out, z_masks)
-        gram, *slots = gather(table, keep, got, gram)
+        made = gather(table, keep, got, gram)
+        gram, slots = (made[0], list(made[1:])) if layer == 0 else (made[:2], list(made[2:]))
         slots = slots[:1] + move_all(slots[1:], chip_masks)
         other = move(pack(slots), core_mask)
         held.append(arrange(table, slots, other))
 
-    for mask in (core_mask, 4, 2, 1, 16):
-        gram = gram + move(gram, mask)
-    return finish(gram, *held, math.sqrt(27 * channels))
+    mine = gram[0] + move(gram[1], core_mask)
+    for masks in (z_masks, chip_masks):
+        one, two, both = move_all([mine] * 3, masks)
+        mine = (mine + one) + (two + both)
+    theirs = move(mine, core_mask)
+    return finish(table, mine, theirs, *held, math.sqrt(27 * channels))
 
 
 def solution(mesh):

time: 125 us -> 122 us (0.976)
  waiting for transfers between devices: 49 us -> 39.4 us
  starting transfers between devices: 44.4 us -> 49.9 us
    ppermute x40 -> x43, waiting for transfers between devices: 49 us -> 39.4 us  [swap(): return lax.ppermute(value, AXES, [(d, d ^ mask) for d in range(total)])]
    ppermute x40 -> x43, starting transfers between devices: 43.7 us -> 49.2 us  [swap(): return lax.ppermute(value, AXES, [(d, d ^ mask) for d in range(total)])]
  transfers between devices with their start and end apart: 41 -> 44, of which waited for: 17 -> 15; matrix products, arithmetic and copies ran while one was open for 2% -> 2% of each run, Pallas kernels for 15% -> 16%
where the time goes in v1:
time: 122 us; the launch traced here: 121 us
  starting transfers between devices  49.9 us (41%)
  waiting for transfers between devices  39.4 us (32%)
  Pallas kernels  28.1 us (23%)
  local copies, waits for them, and re-layouts  1.63 us (1%)
  matrix products  1.5 us (1%)
    ppermute x43, starting transfers between devices, swap(): return lax.ppermute(value, AXES, [(d, d ^ mask) for d in range(total)])  49.2 us
    ppermute x43, waiting for transfers between devices, swap(): return lax.ppermute(value, AXES, [(d, d ^ mask) for d in range(total)])  39.4 us
    pallas_call x2, Pallas kernels, plane(): pl.pallas_call(functools.partial(plane_kernel, frames, widths, rank), in_...  13.4 us
    pallas_call x1, Pallas kernels, finish(): pl.pallas_call(functools.partial(finish_kernel, size, scale), in_specs=[p...  7.59 us
    pallas_call x2, Pallas kernels, turn(): pl.pallas_call(functools.partial(turn_kernel, frames, positions // frames...  2.94 us
  transfers between devices with their start and end apart: 44, of which 15 were waited for; matrix products, arithmetic and copies ran while one was open for 2% of the time, Pallas kernels for 16%

profile of v1, /device:TPU:0, one launch (start us, length us, event | category | flops | bytes accessed | tf_op | source)
XLA Modules:
  0.0 121.5 jit_solution(17280086145603159679)
XLA Ops:
  0.0 0.5 collective-permute-start
  0.5 0.9 copy-done
  1.4 1.5 %convolution_convert_fusion = bf16[1024,128]{1,0:T(8,128)(2,1)S(1)} fusion(bf16[1024,768]{1,0:T(8,128)(2,1)S(1)} %bitcast.19, bf16[768,128]{1,0:T(8,128)(2,1)} %param.6), kind=kOutput, calls=%fused_computation | convolution fusion | flops 201457664 | bytes 2031616 | tf_op jit(solution)/shard_map/dot_general | solution.py:528
  2.9 0.7 fusion.1
  3.6 0.7 collective-permute-start.4
  4.3 0.7 constant_dynamic-slice_fusion
  5.0 0.6 pieces.1
  5.6 9.9 %collective-permute-start.18 = (bf16[8,3,32,128]{3,2,1,0:T(8,128)(2,1)S(1)}, bf16[8,3,32,128]{3,2,1,0:T(8,128)(2,1)S(1)}, u32[]{:S(2)}, u32[]{:S(2)}) collective-permute-start(bf16[8,3,32,128]{3,2,1,0:T(8,128)(2,1)S(1)} %get-tuple-element.47.refs_4_), channel_id=1, source_target_pairs={{0,1},{1,0},{2,3},{3,2},{4,5},{5,4},{6,7},{7,6},{8,9},{9,8},{10,11... | collective-permute-start | bytes 589832 | tf_op jit(solution)/shard_map/ppermute | solution.py:19
  15.4 1.5 %collective-permute-start.19 = (bf16[8,3,32,128]{3,2,1,0:T(8,128)(2,1)S(1)}, bf16[8,3,32,128]{3,2,1,0:T(8,128)(2,1)S(1)}, u32[]{:S(2)}, u32[]{:S(2)}) collective-permute-start(bf16[8,3,32,128]{3,2,1,0:T(8,128)(2,1)S(1)} %get-tuple-element.47.refs_4_), channel_id=1, source_target_pairs={{0,16},{1,17},{2,18},{3,19},{4,20},{5,21},{6,22},{7,23},{8,24},{9,... | collective-permute-start | bytes 589832 | tf_op jit(solution)/shard_map/ppermute | solution.py:19
  17.0 0.0 collective-permute-start.20
  17.0 4.1 %collective-permute-done.18.refs_5_ = bf16[8,3,32,128]{3,2,1,0:T(8,128)(2,1)S(1)} collective-permute-done((bf16[8,3,32,128]{3,2,1,0:T(8,128)(2,1)S(1)}, bf16[8,3,32,128]{3,2,1,0:T(8,128)(2,1)S(1)}, u32[]{:S(2)}, u32[]{:S(2)}) %collective-permute-start.18) | collective-permute-done | bytes 196640 | tf_op jit(solution)/shard_map/ppermute | solution.py:19
  21.0 1.5 %collective-permute-start.6 = (bf16[8,3,32,128]{3,2,1,0:T(8,128)(2,1)S(1)}, bf16[8,3,32,128]{3,2,1,0:T(8,128)(2,1)S(1)}, u32[]{:S(2)}, u32[]{:S(2)}) collective-permute-start(bf16[8,3,32,128]{3,2,1,0:T(8,128)(2,1)S(1)} %get-tuple-element.38.refs_4_), channel_id=1, source_target_pairs={{0,16},{1,17},{2,18},{3,19},{4,20},{5,21},{6,22},{7,23},{8,24},{9,... | collective-permute-start | bytes 589832 | tf_op jit(solution)/shard_map/ppermute | solution.py:19
  22.6 6.2 %collective-permute-done.19.refs_6_ = bf16[8,3,32,128]{3,2,1,0:T(8,128)(2,1)S(1)} collective-permute-done((bf16[8,3,32,128]{3,2,1,0:T(8,128)(2,1)S(1)}, bf16[8,3,32,128]{3,2,1,0:T(8,128)(2,1)S(1)}, u32[]{:S(2)}, u32[]{:S(2)}) %collective-permute-start.19) | collective-permute-done | bytes 196640 | tf_op jit(solution)/shard_map/ppermute | solution.py:19
  28.7 0.5 collective-permute-start.7
  29.3 2.7 %collective-permute-start.5 = (bf16[8,3,32,128]{3,2,1,0:T(8,128)(2,1)S(1)}, bf16[8,3,32,128]{3,2,1,0:T(8,128)(2,1)S(1)}, u32[]{:S(2)}, u32[]{:S(2)}) collective-permute-start(bf16[8,3,32,128]{3,2,1,0:T(8,128)(2,1)S(1)} %get-tuple-element.38.refs_4_), channel_id=1, source_target_pairs={{0,1},{1,0},{2,3},{3,2},{4,5},{5,4},{6,7},{7,6},{8,9},{9,8},{10,11... | collective-permute-start | bytes 589832 | tf_op jit(solution)/shard_map/ppermute | solution.py:19
  32.0 0.5 collective-permute-start.22
  32.5 0.1 collective-permute-start.23
  32.5 1.5 %turn.3 = (bf16[96,1024]{1,0:T(8,128)(2,1)S(1)}, bf16[96,1024]{1,0:T(8,128)(2,1)S(1)}, bf16[96,1024]{1,0:T(8,128)(2,1)S(1)}, bf16[96,1024]{1,0:T(8,128)(2,1)S(1)}) custom-call(s32[174]{0:T(256)S(1)} %bitcast.27, bf16[2,512,768]{2,1,0:T(8,128)(2,1)S(1)} %bitcast.21, bf16[2,512,768]{2,1,0:T(8,128)(2,1)} %collective-permute-done.got_ref), custom_call_target="tpu_custom_call" | custom-call | bytes 1572864 | tf_op jit(solution)/shard_map/turn/pallas_call | solution.py:305
  34.0 1.3 %collective-permute-done.7.refs_7_ = bf16[8,3,32,128]{3,2,1,0:T(8,128)(2,1)S(1)} collective-permute-done((bf16[8,3,32,128]{3,2,1,0:T(8,128)(2,1)S(1)}, bf16[8,3,32,128]{3,2,1,0:T(8,128)(2,1)S(1)}, u32[]{:S(2)}, u32[]{:S(2)}) %collective-permute-start.7) | collective-permute-done | bytes 196640 | tf_op jit(solution)/shard_map/ppermute | solution.py:19
  35.3 2.4 %collective-permute-done.5.refs_5_ = bf16[8,3,32,128]{3,2,1,0:T(8,128)(2,1)S(1)} collective-permute-done((bf16[8,3,32,128]{3,2,1,0:T(8,128)(2,1)S(1)}, bf16[8,3,32,128]{3,2,1,0:T(8,128)(2,1)S(1)}, u32[]{:S(2)}, u32[]{:S(2)}) %collective-permute-start.5) | collective-permute-done | bytes 196640 | tf_op jit(solution)/shard_map/ppermute | solution.py:19
  37.7 0.6 collective-permute-start.16
  38.3 2.9 %collective-permute-start.17 = (bf16[96,1024]{1,0:T(8,128)(2,1)S(1)}, bf16[96,1024]{1,0:T(8,128)(2,1)S(1)}, u32[]{:S(2)}, u32[]{:S(2)}) collective-permute-start(bf16[96,1024]{1,0:T(8,128)(2,1)S(1)} %get-tuple-element.46), channel_id=1, source_target_pairs={{0,17},{1,16},{2,19},{3,18},{4,21},{5,20},{6,23},{7,22},{8,25},{9,... | collective-permute-start | bytes 589832 | tf_op jit(solution)/shard_map/ppermute | solution.py:19
  41.2 1.5 %turn.2 = (bf16[96,1024]{1,0:T(8,128)(2,1)S(1)}, bf16[96,1024]{1,0:T(8,128)(2,1)S(1)}, bf16[96,1024]{1,0:T(8,128)(2,1)S(1)}, bf16[96,1024]{1,0:T(8,128)(2,1)S(1)}) custom-call(s32[174]{0:T(256)S(1)} %bitcast.28, bf16[2,512,768]{2,1,0:T(8,128)(2,1)S(1)} %bitcast.22, bf16[2,512,768]{2,1,0:T(8,128)(2,1)} %collective-permute-done.got_ref), custom_call_target="tpu_custom_call" | custom-call | bytes 1572864 | tf_op jit(solution)/shard_map/turn/pallas_call | solution.py:305
  42.7 0.1 collective-permute-start.11
  42.8 0.5 collective-permute-start.9
  43.3 2.2 %collective-permute-done.15.refs_1_ = bf16[96,1024]{1,0:T(8,128)(2,1)S(1)} collective-permute-done((bf16[96,1024]{1,0:T(8,128)(2,1)S(1)}, bf16[96,1024]{1,0:T(8,128)(2,1)S(1)}, u32[]{:S(2)}, u32[]{:S(2)}) %collective-permute-start.15) | collective-permute-done | bytes 196640 | tf_op jit(solution)/shard_map/ppermute | solution.py:19
  45.5 4.1 %collective-permute-done.16.refs_2_ = bf16[96,1024]{1,0:T(8,128)(2,1)S(1)} collective-permute-done((bf16[96,1024]{1,0:T(8,128)(2,1)S(1)}, bf16[96,1024]{1,0:T(8,128)(2,1)S(1)}, u32[]{:S(2)}, u32[]{:S(2)}) %collective-permute-start.16) | collective-permute-done | bytes 196640 | tf_op jit(solution)/shard_map/ppermute | solution.py:19
  49.6 2.9 %collective-permute-start.3 = (bf16[96,1024]{1,0:T(8,128)(2,1)S(1)}, bf16[96,1024]{1,0:T(8,128)(2,1)S(1)}, u32[]{:S(2)}, u32[]{:S(2)}) collective-permute-start(bf16[96,1024]{1,0:T(8,128)(2,1)S(1)} %get-tuple-element.37), channel_id=1, source_target_pairs={{0,17},{1,16},{2,19},{3,18},{4,21},{5,20},{6,23},{7,22},{8,25},{9,... | collective-permute-start | bytes 589832 | tf_op jit(solution)/shard_map/ppermute | solution.py:19
  52.4 6.8 %plane.3 = (f32[28,24,128]{2,1,0:T(8,128)S(1)}, bf16[28,24,128]{2,1,0:T(8,128)(2,1)S(1)}, bf16[28,24,128]{2,1,0:T(8,128)(2,1)S(1)}, bf16[28,24,128]{2,1,0:T(8,128)(2,1)S(1)}) custom-call(s32[174]{0:T(256)S(1)} %bitcast.29, bf16[96,1024]{1,0:T(8,128)(2,1)S(1)} %get-tuple-element.43.refs_0_, bf16[96,1024]{1,0:T(8,128)(2,1)S(1)} %collective-permute-done.15.refs_1_, ...), custom_call_target="tpu_custom_call" | custom-call | flops 2717908992 | bytes 6291456 | tf_op jit(solution)/shard_map/plane/pallas_call | solution.py:396
  59.2 1.6 %collective-permute-start.25 = (bf16[28,24,128]{2,1,0:T(8,128)(2,1)S(1)}, bf16[28,24,128]{2,1,0:T(8,128)(2,1)S(1)}, u32[]{:S(2)}, u32[]{:S(2)}) collective-permute-start(bf16[28,24,128]{2,1,0:T(8,128)(2,1)S(1)} %get-tuple-element.49), channel_id=1, source_target_pairs={{0,2},{1,3},{2,0},{3,1},{4,6},{5,7},{6,4},{7,5},{8,10},{9,11},{10,... | collective-permute-start | bytes 516104 | tf_op jit(solution)/shard_map/ppermute | solution.py:19
  60.9 1.7 %collective-permute-start.26 = (bf16[28,24,128]{2,1,0:T(8,128)(2,1)S(1)}, bf16[28,24,128]{2,1,0:T(8,128)(2,1)S(1)}, u32[]{:S(2)}, u32[]{:S(2)}) collective-permute-start(bf16[28,24,128]{2,1,0:T(8,128)(2,1)S(1)} %get-tuple-element.50), channel_id=1, source_target_pairs={{0,4},{1,5},{2,6},{3,7},{4,0},{5,1},{6,2},{7,3},{8,12},{9,13},{10,... | collective-permute-start | bytes 516104 | tf_op jit(solution)/shard_map/ppermute | solution.py:19
  62.6 1.1 collective-permute-start.27
  63.7 6.6 %plane.2 = (f32[28,24,128]{2,1,0:T(8,128)S(1)}, bf16[28,24,128]{2,1,0:T(8,128)(2,1)S(1)}, bf16[28,24,128]{2,1,0:T(8,128)(2,1)S(1)}, bf16[28,24,128]{2,1,0:T(8,128)(2,1)S(1)}) custom-call(s32[174]{0:T(256)S(1)} %bitcast.30, bf16[96,1024]{1,0:T(8,128)(2,1)S(1)} %get-tuple-element.34.refs_0_, bf16[96,1024]{1,0:T(8,128)(2,1)S(1)} %collective-permute-done.1.refs_1_, ...), custom_call_target="tpu_custom_call" | custom-call | flops 2717908992 | bytes 6291456 | tf_op jit(solution)/shard_map/plane/pallas_call | solution.py:396
  70.3 0.7 collective-permute-start.12
  71.0 2.6 %collective-permute-start.13 = (bf16[28,24,128]{2,1,0:T(8,128)(2,1)S(1)}, bf16[28,24,128]{2,1,0:T(8,128)(2,1)S(1)}, u32[]{:S(2)}, u32[]{:S(2)}) collective-permute-start(bf16[28,24,128]{2,1,0:T(8,128)(2,1)S(1)} %get-tuple-element.41), channel_id=1, source_target_pairs={{0,4},{1,5},{2,6},{3,7},{4,0},{5,1},{6,2},{7,3},{8,12},{9,13},{10,... | collective-permute-start | bytes 516104 | tf_op jit(solution)/shard_map/ppermute | solution.py:19
  73.7 1.1 collective-permute-start.14
  74.8 1.2 collective-permute-done.26.refs_2_
  76.0 1.1 gather.2
  77.1 1.4 %collective-permute-done.12.refs_1_ = bf16[28,24,128]{2,1,0:T(8,128)(2,1)S(1)} collective-permute-done((bf16[28,24,128]{2,1,0:T(8,128)(2,1)S(1)}, bf16[28,24,128]{2,1,0:T(8,128)(2,1)S(1)}, u32[]{:S(2)}, u32[]{:S(2)}) %collective-permute-start.12) | collective-permute-done | bytes 172064 | tf_op jit(solution)/shard_map/ppermute | solution.py:19
  78.5 12.1 %collective-permute-done.13.refs_2_ = bf16[28,24,128]{2,1,0:T(8,128)(2,1)S(1)} collective-permute-done((bf16[28,24,128]{2,1,0:T(8,128)(2,1)S(1)}, bf16[28,24,128]{2,1,0:T(8,128)(2,1)S(1)}, u32[]{:S(2)}, u32[]{:S(2)}) %collective-permute-start.13) | collective-permute-done | bytes 172064 | tf_op jit(solution)/shard_map/ppermute | solution.py:19
  90.6 1.1 gather.3
  91.7 0.5 collective-permute-start.40
  92.2 1.2 collective-permute-done.28
  93.4 2.5 %collective-permute-start.29 = (f32[72,128]{1,0:T(8,128)S(1)}, f32[72,128]{1,0:T(8,128)S(1)}, u32[]{:S(2)}, u32[]{:S(2)}) collective-permute-start(f32[72,128]{1,0:T(8,128)S(1)} %add.30), channel_id=1, source_target_pairs={{0,2},{1,3},{2,0},{3,1},{4,6},{5,7},{6,4},{7,5},{8,10},{9,11},{10,... | collective-permute-start | bytes 110600 | tf_op jit(solution)/shard_map/ppermute | solution.py:19
  95.9 1.1 collective-permute-start.30
  97.0 1.4 %collective-permute-start.31 = (f32[72,128]{1,0:T(8,128)S(1)}, f32[72,128]{1,0:T(8,128)S(1)}, u32[]{:S(2)}, u32[]{:S(2)}) collective-permute-start(f32[72,128]{1,0:T(8,128)S(1)} %add.30), channel_id=1, source_target_pairs={{0,6},{1,7},{2,4},{3,5},{4,2},{5,3},{6,0},{7,1},{8,14},{9,15},{10,... | collective-permute-start | bytes 110600 | tf_op jit(solution)/shard_map/ppermute | solution.py:19
  98.3 0.4 collective-permute-start.41
  98.7 2.6 %collective-permute-start.42 = (f32[2,4,24,128]{3,2,1,0:T(8,128)S(1)}, f32[2,4,24,128]{3,2,1,0:T(8,128)S(1)}, u32[]{:S(2)}, u32[]{:S(2)}) collective-permute-start(f32[2,4,24,128]{3,2,1,0:T(8,128)S(1)} %get-tuple-element.62), channel_id=1, source_target_pairs={{0,17},{1,16},{2,19},{3,18},{4,21},{5,20},{6,23},{7,22},{8,25},{9,... | collective-permute-start | bytes 294920 | tf_op jit(solution)/shard_map/ppermute | solution.py:19
  101.4 0.5 collective-permute-done.30
  101.9 1.5 %collective-permute-start.36 = (f32[2,4,24,128]{3,2,1,0:T(8,128)S(1)}, f32[2,4,24,128]{3,2,1,0:T(8,128)S(1)}, u32[]{:S(2)}, u32[]{:S(2)}) collective-permute-start(f32[2,4,24,128]{3,2,1,0:T(8,128)S(1)} %get-tuple-element.56), channel_id=1, source_target_pairs={{0,1},{1,0},{2,3},{3,2},{4,5},{5,4},{6,7},{7,6},{8,9},{9,8},{10,11... | collective-permute-start | bytes 294920 | tf_op jit(solution)/shard_map/ppermute | solution.py:19
  103.4 0.3 collective-permute-start.37
  103.7 2.0 %collective-permute-start.38 = (f32[2,4,24,128]{3,2,1,0:T(8,128)S(1)}, f32[2,4,24,128]{3,2,1,0:T(8,128)S(1)}, u32[]{:S(2)}, u32[]{:S(2)}) collective-permute-start(f32[2,4,24,128]{3,2,1,0:T(8,128)S(1)} %get-tuple-element.58), channel_id=1, source_target_pairs={{0,17},{1,16},{2,19},{3,18},{4,21},{5,20},{6,23},{7,22},{8,25},{9,... | collective-permute-start | bytes 294920 | tf_op jit(solution)/shard_map/ppermute | solution.py:19
  105.7 1.2 %collective-permute-start.32 = (f32[72,128]{1,0:T(8,128)S(1)}, f32[72,128]{1,0:T(8,128)S(1)}, u32[]{:S(2)}, u32[]{:S(2)}) collective-permute-start(f32[72,128]{1,0:T(8,128)S(1)} %add_add_fusion.1), channel_id=1, source_target_pairs={{0,1},{1,0},{2,3},{3,2},{4,5},{5,4},{6,7},{7,6},{8,9},{9,8},{10,11... | collective-permute-start | bytes 110600 | tf_op jit(solution)/shard_map/ppermute | solution.py:19
  107.0 0.3 collective-permute-start.33
  107.3 0.3 collective-permute-done.36.s1
  107.5 1.8 %collective-permute-start.34 = (f32[72,128]{1,0:T(8,128)S(1)}, f32[72,128]{1,0:T(8,128)S(1)}, u32[]{:S(2)}, u32[]{:S(2)}) collective-permute-start(f32[72,128]{1,0:T(8,128)S(1)} %add_add_fusion.1), channel_id=1, source_target_pairs={{0,17},{1,16},{2,19},{3,18},{4,21},{5,20},{6,23},{7,22},{8,25},{9,... | collective-permute-start | bytes 110600 | tf_op jit(solution)/shard_map/ppermute | solution.py:19
  109.3 0.6 collective-permute-done.37.s2
  109.9 0.6 collective-permute-start.39
  110.5 0.4 collective-permute-done.33
  110.9 1.4 %collective-permute-done.34 = f32[72,128]{1,0:T(8,128)S(1)} collective-permute-done((f32[72,128]{1,0:T(8,128)S(1)}, f32[72,128]{1,0:T(8,128)S(1)}, u32[]{:S(2)}, u32[]{:S(2)}) %collective-permute-start.34) | collective-permute-done | bytes 36896 | tf_op jit(solution)/shard_map/ppermute | solution.py:19
  112.4 0.1 collective-permute-start.35
  112.5 0.7 arrange.3.second_ref
  113.2 0.7 arrange.2.first_ref
  113.9 7.6 %finish.1 = f32[2,648,128]{2,1,0:T(8,128)} custom-call(s32[174]{0:T(256)S(1)} %bitcast.35, f32[72,128]{1,0:T(8,128)S(1)} %add_add_fusion.mine_ref, f32[72,128]{1,0:T(8,128)S(1)} %collective-permute-done.35.theirs_ref, bf16[648,768]{1,0:T(8,128)(2,1)S(1)} %arrange.2.first_ref, bf16[648,768]{1,0:T(8,128)(2,1)S(1)} %arrange.3.second_ref), custom_call_target="tpu_custom_call" | custom-call | flops 2147483648 | bytes 4194304 | tf_op jit(solution)/shard_map/finish/pallas_call | solution.py:171
  (46 shorter events, 0.2 us)
Async XLA Ops:
  0.0 1.4 %copy-start = (bf16[2,1,8,2,32,768]{5,4,3,2,1,0:T(8,128)(2,1)S(1)}, bf16[2,1,8,2,32,768]{5,4,3,2,1,0:T(8,128)(2,1)}, u32[]{:S(2)}) copy-start(bf16[2,1,8,2,32,768]{5,4,3,2,1,0:T(8,128)(2,1)} %param.5) | copy-start | bytes 4718596
  0.0 32.5 %copy-start.1 = (bf16[2,1,8,2,32,768]{5,4,3,2,1,0:T(8,128)(2,1)S(1)}, bf16[2,1,8,2,32,768]{5,4,3,2,1,0:T(8,128)(2,1)}, u32[]{:S(2)}) copy-start(bf16[2,1,8,2,32,768]{5,4,3,2,1,0:T(8,128)(2,1)} %param.4) | copy-start | bytes 4718596
  0.0 32.5 %collective-permute-start = (bf16[2,512,768]{2,1,0:T(8,128)(2,1)}, bf16[2,512,768]{2,1,0:T(8,128)(2,1)}, u32[]{:S(2)}, u32[]{:S(2)}) collective-permute-start(bf16[2,512,768]{2,1,0:T(8,128)(2,1)} %bitcast.20), channel_id=1, source_target_pairs={{0,8},{1,9},{2,10},{3,11},{4,12},{5,13},{6,14},{7,15},{8,0},{9,1},... | collective-permute-start | bytes 4718600 | tf_op jit(solution)/shard_map/ppermute | solution.py:19
  3.6 1.4 %collective-permute-start.4 = (bf16[2,8,32,128]{3,2,1,0:T(8,128)(2,1)}, bf16[2,8,32,128]{3,2,1,0:T(8,128)(2,1)S(1)}, u32[]{:S(2)}, u32[]{:S(2)}) collective-permute-start(bf16[2,8,32,128]{3,2,1,0:T(8,128)(2,1)} %fusion.1), channel_id=1, source_target_pairs={{1,2},{3,4},{5,6},{2,1},{4,3},{6,5},{9,10},{11,12},{13,14},{10,9},... | collective-permute-start | bytes 393224 | tf_op jit(solution)/shard_map/ppermute | solution.py:532
  5.6 15.5 %collective-permute-start.18 = (bf16[8,3,32,128]{3,2,1,0:T(8,128)(2,1)S(1)}, bf16[8,3,32,128]{3,2,1,0:T(8,128)(2,1)S(1)}, u32[]{:S(2)}, u32[]{:S(2)}) collective-permute-start(bf16[8,3,32,128]{3,2,1,0:T(8,128)(2,1)S(1)} %get-tuple-element.47.refs_4_), channel_id=1, source_target_pairs={{0,1},{1,0},{2,3},{3,2},{4,5},{5,4},{6,7},{7,6},{8,9},{9,8},{10,11... | collective-permute-start | bytes 589832 | tf_op jit(solution)/shard_map/ppermute | solution.py:19
  15.4 13.3 %collective-permute-start.19 = (bf16[8,3,32,128]{3,2,1,0:T(8,128)(2,1)S(1)}, bf16[8,3,32,128]{3,2,1,0:T(8,128)(2,1)S(1)}, u32[]{:S(2)}, u32[]{:S(2)}) collective-permute-start(bf16[8,3,32,128]{3,2,1,0:T(8,128)(2,1)S(1)} %get-tuple-element.47.refs_4_), channel_id=1, source_target_pairs={{0,16},{1,17},{2,18},{3,19},{4,20},{5,21},{6,22},{7,23},{8,24},{9,... | collective-permute-start | bytes 589832 | tf_op jit(solution)/shard_map/ppermute | solution.py:19
  17.0 12.3 %collective-permute-start.20 = (bf16[8,3,32,128]{3,2,1,0:T(8,128)(2,1)S(1)}, bf16[8,3,32,128]{3,2,1,0:T(8,128)(2,1)S(1)}, u32[]{:S(2)}, u32[]{:S(2)}) collective-permute-start(bf16[8,3,32,128]{3,2,1,0:T(8,128)(2,1)S(1)} %get-tuple-element.47.refs_4_), channel_id=1, source_target_pairs={{0,17},{1,16},{2,19},{3,18},{4,21},{5,20},{6,23},{7,22},{8,25},{9,... | collective-permute-start | bytes 589832 | tf_op jit(solution)/shard_map/ppermute | solution.py:19
  17.0 15.0 %collective-permute-start.21 = (bf16[8,3,32,128]{3,2,1,0:T(8,128)(2,1)S(1)}, bf16[8,3,32,128]{3,2,1,0:T(8,128)(2,1)S(1)}, u32[]{:S(2)}, u32[]{:S(2)}) collective-permute-start(bf16[8,3,32,128]{3,2,1,0:T(8,128)(2,1)S(1)} %get-tuple-element.47.refs_4_), channel_id=1, source_target_pairs={{0,8},{1,9},{2,10},{3,11},{4,12},{5,13},{6,14},{7,15},{8,0},{9,1},... | collective-permute-start | bytes 589832 | tf_op jit(solution)/shard_map/ppermute | solution.py:19
  21.0 10.9 %collective-permute-start.6 = (bf16[8,3,32,128]{3,2,1,0:T(8,128)(2,1)S(1)}, bf16[8,3,32,128]{3,2,1,0:T(8,128)(2,1)S(1)}, u32[]{:S(2)}, u32[]{:S(2)}) collective-permute-start(bf16[8,3,32,128]{3,2,1,0:T(8,128)(2,1)S(1)} %get-tuple-element.38.refs_4_), channel_id=1, source_target_pairs={{0,16},{1,17},{2,18},{3,19},{4,20},{5,21},{6,22},{7,23},{8,24},{9,... | collective-permute-start | bytes 589832 | tf_op jit(solution)/shard_map/ppermute | solution.py:19
  28.7 6.6 %collective-permute-start.7 = (bf16[8,3,32,128]{3,2,1,0:T(8,128)(2,1)S(1)}, bf16[8,3,32,128]{3,2,1,0:T(8,128)(2,1)S(1)}, u32[]{:S(2)}, u32[]{:S(2)}) collective-permute-start(bf16[8,3,32,128]{3,2,1,0:T(8,128)(2,1)S(1)} %get-tuple-element.38.refs_4_), channel_id=1, source_target_pairs={{0,17},{1,16},{2,19},{3,18},{4,21},{5,20},{6,23},{7,22},{8,25},{9,... | collective-permute-start | bytes 589832 | tf_op jit(solution)/shard_map/ppermute | solution.py:19
  29.3 8.4 %collective-permute-start.5 = (bf16[8,3,32,128]{3,2,1,0:T(8,128)(2,1)S(1)}, bf16[8,3,32,128]{3,2,1,0:T(8,128)(2,1)S(1)}, u32[]{:S(2)}, u32[]{:S(2)}) collective-permute-start(bf16[8,3,32,128]{3,2,1,0:T(8,128)(2,1)S(1)} %get-tuple-element.38.refs_4_), channel_id=1, source_target_pairs={{0,1},{1,0},{2,3},{3,2},{4,5},{5,4},{6,7},{7,6},{8,9},{9,8},{10,11... | collective-permute-start | bytes 589832 | tf_op jit(solution)/shard_map/ppermute | solution.py:19
  31.9 5.7 %collective-permute-start.8 = (bf16[8,3,32,128]{3,2,1,0:T(8,128)(2,1)S(1)}, bf16[8,3,32,128]{3,2,1,0:T(8,128)(2,1)S(1)}, u32[]{:S(2)}, u32[]{:S(2)}) collective-permute-start(bf16[8,3,32,128]{3,2,1,0:T(8,128)(2,1)S(1)} %get-tuple-element.38.refs_4_), channel_id=1, source_target_pairs={{0,8},{1,9},{2,10},{3,11},{4,12},{5,13},{6,14},{7,15},{8,0},{9,1},... | collective-permute-start | bytes 589832 | tf_op jit(solution)/shard_map/ppermute | solution.py:19
  32.0 5.8 %collective-permute-start.22 = (bf16[8,3,32,128]{3,2,1,0:T(8,128)(2,1)S(1)}, bf16[8,3,32,128]{3,2,1,0:T(8,128)(2,1)S(1)}, u32[]{:S(2)}, u32[]{:S(2)}) collective-permute-start(bf16[8,3,32,128]{3,2,1,0:T(8,128)(2,1)S(1)} %collective-permute-done.18.refs_5_), channel_id=1, source_target_pairs={{0,8},{1,9},{2,10},{3,11},{4,12},{5,13},{6,14},{7,15},{8,0},{9,1},... | collective-permute-start | bytes 589832 | tf_op jit(solution)/shard_map/ppermute | solution.py:19
  32.5 5.8 %collective-permute-start.23 = (bf16[8,3,32,128]{3,2,1,0:T(8,128)(2,1)S(1)}, bf16[8,3,32,128]{3,2,1,0:T(8,128)(2,1)S(1)}, u32[]{:S(2)}, u32[]{:S(2)}) collective-permute-start(bf16[8,3,32,128]{3,2,1,0:T(8,128)(2,1)S(1)} %collective-permute-done.19.refs_6_), channel_id=1, source_target_pairs={{0,8},{1,9},{2,10},{3,11},{4,12},{5,13},{6,14},{7,15},{8,0},{9,1},... | collective-permute-start | bytes 589832 | tf_op jit(solution)/shard_map/ppermute | solution.py:19
  35.3 7.4 %collective-permute-start.24 = (bf16[8,3,32,128]{3,2,1,0:T(8,128)(2,1)S(1)}, bf16[8,3,32,128]{3,2,1,0:T(8,128)(2,1)S(1)}, u32[]{:S(2)}, u32[]{:S(2)}) collective-permute-start(bf16[8,3,32,128]{3,2,1,0:T(8,128)(2,1)S(1)} %collective-permute-done.20.refs_7_), channel_id=1, source_target_pairs={{0,8},{1,9},{2,10},{3,11},{4,12},{5,13},{6,14},{7,15},{8,0},{9,1},... | collective-permute-start | bytes 589832 | tf_op jit(solution)/shard_map/ppermute | solution.py:19
  37.7 5.1 %collective-permute-start.10 = (bf16[8,3,32,128]{3,2,1,0:T(8,128)(2,1)S(1)}, bf16[8,3,32,128]{3,2,1,0:T(8,128)(2,1)S(1)}, u32[]{:S(2)}, u32[]{:S(2)}) collective-permute-start(bf16[8,3,32,128]{3,2,1,0:T(8,128)(2,1)S(1)} %collective-permute-done.6.refs_6_), channel_id=1, source_target_pairs={{0,8},{1,9},{2,10},{3,11},{4,12},{5,13},{6,14},{7,15},{8,0},{9,1},... | collective-permute-start | bytes 589832 | tf_op jit(solution)/shard_map/ppermute | solution.py:19
  37.7 7.8 %collective-permute-start.15 = (bf16[96,1024]{1,0:T(8,128)(2,1)S(1)}, bf16[96,1024]{1,0:T(8,128)(2,1)S(1)}, u32[]{:S(2)}, u32[]{:S(2)}) collective-permute-start(bf16[96,1024]{1,0:T(8,128)(2,1)S(1)} %get-tuple-element.44), channel_id=1, source_target_pairs={{0,1},{1,0},{2,3},{3,2},{4,5},{5,4},{6,7},{7,6},{8,9},{9,8},{10,11... | collective-permute-start | bytes 589832 | tf_op jit(solution)/shard_map/ppermute | solution.py:19
  37.7 11.8 %collective-permute-start.16 = (bf16[96,1024]{1,0:T(8,128)(2,1)S(1)}, bf16[96,1024]{1,0:T(8,128)(2,1)S(1)}, u32[]{:S(2)}, u32[]{:S(2)}) collective-permute-start(bf16[96,1024]{1,0:T(8,128)(2,1)S(1)} %get-tuple-element.45), channel_id=1, source_target_pairs={{0,16},{1,17},{2,18},{3,19},{4,20},{5,21},{6,22},{7,23},{8,24},{9,... | collective-permute-start | bytes 589832 | tf_op jit(solution)/shard_map/ppermute | solution.py:19
  38.3 11.3 %collective-permute-start.17 = (bf16[96,1024]{1,0:T(8,128)(2,1)S(1)}, bf16[96,1024]{1,0:T(8,128)(2,1)S(1)}, u32[]{:S(2)}, u32[]{:S(2)}) collective-permute-start(bf16[96,1024]{1,0:T(8,128)(2,1)S(1)} %get-tuple-element.46), channel_id=1, source_target_pairs={{0,17},{1,16},{2,19},{3,18},{4,21},{5,20},{6,23},{7,22},{8,25},{9,... | collective-permute-start | bytes 589832 | tf_op jit(solution)/shard_map/ppermute | solution.py:19
  42.7 16.5 %collective-permute-start.11 = (bf16[8,3,32,128]{3,2,1,0:T(8,128)(2,1)S(1)}, bf16[8,3,32,128]{3,2,1,0:T(8,128)(2,1)S(1)}, u32[]{:S(2)}, u32[]{:S(2)}) collective-permute-start(bf16[8,3,32,128]{3,2,1,0:T(8,128)(2,1)S(1)} %collective-permute-done.7.refs_7_), channel_id=1, source_target_pairs={{0,8},{1,9},{2,10},{3,11},{4,12},{5,13},{6,14},{7,15},{8,0},{9,1},... | collective-permute-start | bytes 589832 | tf_op jit(solution)/shard_map/ppermute | solution.py:19
  42.8 18.1 %collective-permute-start.9 = (bf16[8,3,32,128]{3,2,1,0:T(8,128)(2,1)S(1)}, bf16[8,3,32,128]{3,2,1,0:T(8,128)(2,1)S(1)}, u32[]{:S(2)}, u32[]{:S(2)}) collective-permute-start(bf16[8,3,32,128]{3,2,1,0:T(8,128)(2,1)S(1)} %collective-permute-done.5.refs_5_), channel_id=1, source_target_pairs={{0,8},{1,9},{2,10},{3,11},{4,12},{5,13},{6,14},{7,15},{8,0},{9,1},... | collective-permute-start | bytes 589832 | tf_op jit(solution)/shard_map/ppermute | solution.py:19
  45.5 17.1 %collective-permute-start.1 = (bf16[96,1024]{1,0:T(8,128)(2,1)S(1)}, bf16[96,1024]{1,0:T(8,128)(2,1)S(1)}, u32[]{:S(2)}, u32[]{:S(2)}) collective-permute-start(bf16[96,1024]{1,0:T(8,128)(2,1)S(1)} %get-tuple-element.35), channel_id=1, source_target_pairs={{0,1},{1,0},{2,3},{3,2},{4,5},{5,4},{6,7},{7,6},{8,9},{9,8},{10,11... | collective-permute-start | bytes 589832 | tf_op jit(solution)/shard_map/ppermute | solution.py:19
  49.6 14.1 %collective-permute-start.2 = (bf16[96,1024]{1,0:T(8,128)(2,1)S(1)}, bf16[96,1024]{1,0:T(8,128)(2,1)S(1)}, u32[]{:S(2)}, u32[]{:S(2)}) collective-permute-start(bf16[96,1024]{1,0:T(8,128)(2,1)S(1)} %get-tuple-element.36), channel_id=1, source_target_pairs={{0,16},{1,17},{2,18},{3,19},{4,20},{5,21},{6,22},{7,23},{8,24},{9,... | collective-permute-start | bytes 589832 | tf_op jit(solution)/shard_map/ppermute | solution.py:19
  49.6 14.1 %collective-permute-start.3 = (bf16[96,1024]{1,0:T(8,128)(2,1)S(1)}, bf16[96,1024]{1,0:T(8,128)(2,1)S(1)}, u32[]{:S(2)}, u32[]{:S(2)}) collective-permute-start(bf16[96,1024]{1,0:T(8,128)(2,1)S(1)} %get-tuple-element.37), channel_id=1, source_target_pairs={{0,17},{1,16},{2,19},{3,18},{4,21},{5,20},{6,23},{7,22},{8,25},{9,... | collective-permute-start | bytes 589832 | tf_op jit(solution)/shard_map/ppermute | solution.py:19
  59.2 14.4 %collective-permute-start.25 = (bf16[28,24,128]{2,1,0:T(8,128)(2,1)S(1)}, bf16[28,24,128]{2,1,0:T(8,128)(2,1)S(1)}, u32[]{:S(2)}, u32[]{:S(2)}) collective-permute-start(bf16[28,24,128]{2,1,0:T(8,128)(2,1)S(1)} %get-tuple-element.49), channel_id=1, source_target_pairs={{0,2},{1,3},{2,0},{3,1},{4,6},{5,7},{6,4},{7,5},{8,10},{9,11},{10,... | collective-permute-start | bytes 516104 | tf_op jit(solution)/shard_map/ppermute | solution.py:19
  60.9 15.1 %collective-permute-start.26 = (bf16[28,24,128]{2,1,0:T(8,128)(2,1)S(1)}, bf16[28,24,128]{2,1,0:T(8,128)(2,1)S(1)}, u32[]{:S(2)}, u32[]{:S(2)}) collective-permute-start(bf16[28,24,128]{2,1,0:T(8,128)(2,1)S(1)} %get-tuple-element.50), channel_id=1, source_target_pairs={{0,4},{1,5},{2,6},{3,7},{4,0},{5,1},{6,2},{7,3},{8,12},{9,13},{10,... | collective-permute-start | bytes 516104 | tf_op jit(solution)/shard_map/ppermute | solution.py:19
  62.6 13.4 %collective-permute-start.27 = (bf16[28,24,128]{2,1,0:T(8,128)(2,1)S(1)}, bf16[28,24,128]{2,1,0:T(8,128)(2,1)S(1)}, u32[]{:S(2)}, u32[]{:S(2)}) collective-permute-start(bf16[28,24,128]{2,1,0:T(8,128)(2,1)S(1)} %get-tuple-element.51), channel_id=1, source_target_pairs={{0,6},{1,7},{2,4},{3,5},{4,2},{5,3},{6,0},{7,1},{8,14},{9,15},{10,... | collective-permute-start | bytes 516104 | tf_op jit(solution)/shard_map/ppermute | solution.py:19
  70.3 8.2 %collective-permute-start.12 = (bf16[28,24,128]{2,1,0:T(8,128)(2,1)S(1)}, bf16[28,24,128]{2,1,0:T(8,128)(2,1)S(1)}, u32[]{:S(2)}, u32[]{:S(2)}) collective-permute-start(bf16[28,24,128]{2,1,0:T(8,128)(2,1)S(1)} %get-tuple-element.40), channel_id=1, source_target_pairs={{0,2},{1,3},{2,0},{3,1},{4,6},{5,7},{6,4},{7,5},{8,10},{9,11},{10,... | collective-permute-start | bytes 516104 | tf_op jit(solution)/shard_map/ppermute | solution.py:19
  71.0 19.6 %collective-permute-start.13 = (bf16[28,24,128]{2,1,0:T(8,128)(2,1)S(1)}, bf16[28,24,128]{2,1,0:T(8,128)(2,1)S(1)}, u32[]{:S(2)}, u32[]{:S(2)}) collective-permute-start(bf16[28,24,128]{2,1,0:T(8,128)(2,1)S(1)} %get-tuple-element.41), channel_id=1, source_target_pairs={{0,4},{1,5},{2,6},{3,7},{4,0},{5,1},{6,2},{7,3},{8,12},{9,13},{10,... | collective-permute-start | bytes 516104 | tf_op jit(solution)/shard_map/ppermute | solution.py:19
  73.7 16.9 %collective-permute-start.14 = (bf16[28,24,128]{2,1,0:T(8,128)(2,1)S(1)}, bf16[28,24,128]{2,1,0:T(8,128)(2,1)S(1)}, u32[]{:S(2)}, u32[]{:S(2)}) collective-permute-start(bf16[28,24,128]{2,1,0:T(8,128)(2,1)S(1)} %get-tuple-element.42), channel_id=1, source_target_pairs={{0,6},{1,7},{2,4},{3,5},{4,2},{5,3},{6,0},{7,1},{8,14},{9,15},{10,... | collective-permute-start | bytes 516104 | tf_op jit(solution)/shard_map/ppermute | solution.py:19
  91.7 11.9 %collective-permute-start.40 = (f32[2,4,24,128]{3,2,1,0:T(8,128)S(1)}, f32[2,4,24,128]{3,2,1,0:T(8,128)S(1)}, u32[]{:S(2)}, u32[]{:S(2)}) collective-permute-start(f32[2,4,24,128]{3,2,1,0:T(8,128)S(1)} %get-tuple-element.60), channel_id=1, source_target_pairs={{0,1},{1,0},{2,3},{3,2},{4,5},{5,4},{6,7},{7,6},{8,9},{9,8},{10,11... | collective-permute-start | bytes 294920 | tf_op jit(solution)/shard_map/ppermute | solution.py:19
  92.2 1.2 collective-permute-start.28
  93.4 5.3 %collective-permute-start.29 = (f32[72,128]{1,0:T(8,128)S(1)}, f32[72,128]{1,0:T(8,128)S(1)}, u32[]{:S(2)}, u32[]{:S(2)}) collective-permute-start(f32[72,128]{1,0:T(8,128)S(1)} %add.30), channel_id=1, source_target_pairs={{0,2},{1,3},{2,0},{3,1},{4,6},{5,7},{6,4},{7,5},{8,10},{9,11},{10,... | collective-permute-start | bytes 110600 | tf_op jit(solution)/shard_map/ppermute | solution.py:19
  95.9 6.0 %collective-permute-start.30 = (f32[72,128]{1,0:T(8,128)S(1)}, f32[72,128]{1,0:T(8,128)S(1)}, u32[]{:S(2)}, u32[]{:S(2)}) collective-permute-start(f32[72,128]{1,0:T(8,128)S(1)} %add.30), channel_id=1, source_target_pairs={{0,4},{1,5},{2,6},{3,7},{4,0},{5,1},{6,2},{7,3},{8,12},{9,13},{10,... | collective-permute-start | bytes 110600 | tf_op jit(solution)/shard_map/ppermute | solution.py:19
  97.0 6.4 %collective-permute-start.31 = (f32[72,128]{1,0:T(8,128)S(1)}, f32[72,128]{1,0:T(8,128)S(1)}, u32[]{:S(2)}, u32[]{:S(2)}) collective-permute-start(f32[72,128]{1,0:T(8,128)S(1)} %add.30), channel_id=1, source_target_pairs={{0,6},{1,7},{2,4},{3,5},{4,2},{5,3},{6,0},{7,1},{8,14},{9,15},{10,... | collective-permute-start | bytes 110600 | tf_op jit(solution)/shard_map/ppermute | solution.py:19
  98.3 7.4 %collective-permute-start.41 = (f32[2,4,24,128]{3,2,1,0:T(8,128)S(1)}, f32[2,4,24,128]{3,2,1,0:T(8,128)S(1)}, u32[]{:S(2)}, u32[]{:S(2)}) collective-permute-start(f32[2,4,24,128]{3,2,1,0:T(8,128)S(1)} %get-tuple-element.61), channel_id=1, source_target_pairs={{0,16},{1,17},{2,18},{3,19},{4,20},{5,21},{6,22},{7,23},{8,24},{9,... | collective-permute-start | bytes 294920 | tf_op jit(solution)/shard_map/ppermute | solution.py:19
  98.7 8.2 %collective-permute-start.42 = (f32[2,4,24,128]{3,2,1,0:T(8,128)S(1)}, f32[2,4,24,128]{3,2,1,0:T(8,128)S(1)}, u32[]{:S(2)}, u32[]{:S(2)}) collective-permute-start(f32[2,4,24,128]{3,2,1,0:T(8,128)S(1)} %get-tuple-element.62), channel_id=1, source_target_pairs={{0,17},{1,16},{2,19},{3,18},{4,21},{5,20},{6,23},{7,22},{8,25},{9,... | collective-permute-start | bytes 294920 | tf_op jit(solution)/shard_map/ppermute | solution.py:19
  101.9 5.7 %collective-permute-start.36 = (f32[2,4,24,128]{3,2,1,0:T(8,128)S(1)}, f32[2,4,24,128]{3,2,1,0:T(8,128)S(1)}, u32[]{:S(2)}, u32[]{:S(2)}) collective-permute-start(f32[2,4,24,128]{3,2,1,0:T(8,128)S(1)} %get-tuple-element.56), channel_id=1, source_target_pairs={{0,1},{1,0},{2,3},{3,2},{4,5},{5,4},{6,7},{7,6},{8,9},{9,8},{10,11... | collective-permute-start | bytes 294920 | tf_op jit(solution)/shard_map/ppermute | solution.py:19
  103.4 6.5 %collective-permute-start.37 = (f32[2,4,24,128]{3,2,1,0:T(8,128)S(1)}, f32[2,4,24,128]{3,2,1,0:T(8,128)S(1)}, u32[]{:S(2)}, u32[]{:S(2)}) collective-permute-start(f32[2,4,24,128]{3,2,1,0:T(8,128)S(1)} %get-tuple-element.57), channel_id=1, source_target_pairs={{0,16},{1,17},{2,18},{3,19},{4,20},{5,21},{6,22},{7,23},{8,24},{9,... | collective-permute-start | bytes 294920 | tf_op jit(solution)/shard_map/ppermute | solution.py:19
  103.7 6.3 %collective-permute-start.38 = (f32[2,4,24,128]{3,2,1,0:T(8,128)S(1)}, f32[2,4,24,128]{3,2,1,0:T(8,128)S(1)}, u32[]{:S(2)}, u32[]{:S(2)}) collective-permute-start(f32[2,4,24,128]{3,2,1,0:T(8,128)S(1)} %get-tuple-element.58), channel_id=1, source_target_pairs={{0,17},{1,16},{2,19},{3,18},{4,21},{5,20},{6,23},{7,22},{8,25},{9,... | collective-permute-start | bytes 294920 | tf_op jit(solution)/shard_map/ppermute | solution.py:19
  105.7 4.8 %collective-permute-start.32 = (f32[72,128]{1,0:T(8,128)S(1)}, f32[72,128]{1,0:T(8,128)S(1)}, u32[]{:S(2)}, u32[]{:S(2)}) collective-permute-start(f32[72,128]{1,0:T(8,128)S(1)} %add_add_fusion.1), channel_id=1, source_target_pairs={{0,1},{1,0},{2,3},{3,2},{4,5},{5,4},{6,7},{7,6},{8,9},{9,8},{10,11... | collective-permute-start | bytes 110600 | tf_op jit(solution)/shard_map/ppermute | solution.py:19
  107.0 4.0 %collective-permute-start.33 = (f32[72,128]{1,0:T(8,128)S(1)}, f32[72,128]{1,0:T(8,128)S(1)}, u32[]{:S(2)}, u32[]{:S(2)}) collective-permute-start(f32[72,128]{1,0:T(8,128)S(1)} %add_add_fusion.1), channel_id=1, source_target_pairs={{0,16},{1,17},{2,18},{3,19},{4,20},{5,21},{6,22},{7,23},{8,24},{9,... | collective-permute-start | bytes 110600 | tf_op jit(solution)/shard_map/ppermute | solution.py:19
  107.5 4.9 %collective-permute-start.34 = (f32[72,128]{1,0:T(8,128)S(1)}, f32[72,128]{1,0:T(8,128)S(1)}, u32[]{:S(2)}, u32[]{:S(2)}) collective-permute-start(f32[72,128]{1,0:T(8,128)S(1)} %add_add_fusion.1), channel_id=1, source_target_pairs={{0,17},{1,16},{2,19},{3,18},{4,21},{5,20},{6,23},{7,22},{8,25},{9,... | collective-permute-start | bytes 110600 | tf_op jit(solution)/shard_map/ppermute | solution.py:19
  109.9 2.6 %collective-permute-start.43 = (f32[4,4,24,128]{3,2,1,0:T(8,128)S(1)}, f32[4,4,24,128]{3,2,1,0:T(8,128)S(1)}, u32[]{:S(2)}, u32[]{:S(2)}) collective-permute-start(f32[4,4,24,128]{3,2,1,0:T(8,128)S(1)} %pack.3), channel_id=1, source_target_pairs={{0,8},{1,9},{2,10},{3,11},{4,12},{5,13},{6,14},{7,15},{8,0},{9,1},... | collective-permute-start | bytes 589832 | tf_op jit(solution)/shard_map/ppermute | solution.py:19
  109.9 3.2 %collective-permute-start.39 = (f32[4,4,24,128]{3,2,1,0:T(8,128)S(1)}, f32[4,4,24,128]{3,2,1,0:T(8,128)S(1)}, u32[]{:S(2)}, u32[]{:S(2)}) collective-permute-start(f32[4,4,24,128]{3,2,1,0:T(8,128)S(1)} %pack.2), channel_id=1, source_target_pairs={{0,8},{1,9},{2,10},{3,11},{4,12},{5,13},{6,14},{7,15},{8,0},{9,1},... | collective-permute-start | bytes 589832 | tf_op jit(solution)/shard_map/ppermute | solution.py:19
  112.4 1.5 %collective-permute-start.35 = (f32[72,128]{1,0:T(8,128)S(1)}, f32[72,128]{1,0:T(8,128)S(1)}, u32[]{:S(2)}, u32[]{:S(2)}) collective-permute-start(f32[72,128]{1,0:T(8,128)S(1)} %add_add_fusion.mine_ref), channel_id=1, source_target_pairs={{0,8},{1,9},{2,10},{3,11},{4,12},{5,13},{6,14},{7,15},{8,0},{9,1},... | collective-permute-start | bytes 110600 | tf_op jit(solution)/shard_map/ppermute | solution.py:19

commit v2 on v1

--- a/solution.py
+++ b/solution.py
@@ -142,7 +142,7 @@
     )(gram)
 
 
-def finish_kernel(size, scale, table_ref, mine_ref, theirs_ref, first_ref, second_ref, out_ref, one, two, high, middle, low):
+def inverses_kernel(size, table_ref, mine_ref, theirs_ref, out_ref, one, two, high, middle, low):
     down = lax.broadcasted_iota(jnp.int32, (size, size), 0)
     across = lax.broadcasted_iota(jnp.int32, (size, size), 1)
     core, half = table_ref[PLACE], size // 2 + 8
@@ -158,26 +158,24 @@
             ref[i, start : start + 8, :] = part
 
     eliminate([first, second], [one, two], put)
-    for i, ref in enumerate((first_ref, second_ref)):
+    for i in range(2):
         d, e, f = (part[i].astype(BF16) for part in (high, middle, low))
-        rhs = jnp.concatenate([d, e, d, f, e, d], axis=1)
-        made = lax.dot_general(ref[...], rhs, (((1,), (1,)), ((), ())), preferred_element_type=F32)
-        out_ref[i] = made * scale
-
-
-def finish(table, mine, theirs, first, second, scale):
+        out_ref[i] = jnp.concatenate([d, e, d, f, e, d], axis=1)
+
+
+def inverses_of_factors(table, mine, theirs):
     size = mine.shape[-1]
     vmem = pl.BlockSpec(memory_space=pltpu.VMEM)
     return pl.pallas_call(
-        functools.partial(finish_kernel, size, scale),
-        in_specs=[pl.BlockSpec(memory_space=pltpu.SMEM)] + [vmem] * 4,
+        functools.partial(inverses_kernel, size),
+        in_specs=[pl.BlockSpec(memory_space=pltpu.SMEM)] + [vmem] * 2,
         out_specs=vmem,
-        out_shape=jax.ShapeDtypeStruct((2, first.shape[0], size), F32),
+        out_shape=jax.ShapeDtypeStruct((2, size, 6 * size), BF16),
         scratch_shapes=[pltpu.VMEM((size, 2 * size), F32)] * 2 + [pltpu.VMEM((2, size, size), F32)] * 3,
-        compiler_params=pltpu.CompilerParams(vmem_limit_bytes=8 * 2**20),
-        cost_estimate=pl.CostEstimate(flops=2**31, bytes_accessed=2**22, transcendentals=0),
-        name="finish",
-    )(table, mine, theirs, first, second)
+        compiler_params=pltpu.CompilerParams(vmem_limit_bytes=4 * 2**20),
+        cost_estimate=pl.CostEstimate(flops=2**30, bytes_accessed=2**20, transcendentals=0),
+        name="inverses",
+    )(table, mine, theirs)
 
 
 def pick(value, index, axis):
@@ -416,14 +414,14 @@
 def gather_kernel(rank, joined, table_ref, *refs):
     (keep_ref, g1, g2, g3), refs = refs[:4], refs[4:]
     first_ref, refs = (refs[0], refs[1:]) if joined else (None, refs)
-    grams, slots, rows = refs[: 1 + joined], refs[1 + joined : 5 + joined], refs[5 + joined]
+    grams, (own_ref, over_ref, rows) = refs[: 1 + joined], refs[1 + joined : 4 + joined]
     total = keep_ref[...] + (g1[...].astype(F32) + g2[...].astype(F32) + g3[...].astype(F32))
     rows[0:UNITS] = total
     rows[UNITS] = jnp.zeros((24, rank), F32)
-    for m, ref in enumerate(slots):
-        for other in range(2):
+    for other, ref in enumerate((own_ref, over_ref)):
+        for m in range(4):
             for s in range(4):
-                ref[other, s] = rows[table_ref[BY_CHIP + 8 * m + 4 * other + s]]
+                ref[m, s] = rows[table_ref[BY_CHIP + 8 * m + 4 * other + s]]
     flat = total.reshape(UNITS * 24, rank)
     gram = lax.dot_general(
         flat, flat, (((0,), (0,)), ((), ())), precision=HIGHEST, preferred_element_type=F32
@@ -453,9 +451,9 @@
     return pl.pallas_call(
         functools.partial(gather_kernel, rank, joined),
         in_specs=[pl.BlockSpec(memory_space=pltpu.SMEM)] + [vmem] * (4 + joined),
-        out_specs=[vmem] * (5 + joined),
+        out_specs=[vmem] * (3 + joined),
         out_shape=[jax.ShapeDtypeStruct(gram, F32)] * (1 + joined)
-        + [jax.ShapeDtypeStruct((2, 4, 24, rank), F32)] * 4,
+        + [jax.ShapeDtypeStruct((4, 4, 24, rank), F32)] * 2,
         scratch_shapes=[pltpu.VMEM((UNITS + 1, 24, rank), F32)] + [pltpu.VMEM((2,) + gram, F32)] * joined,
         compiler_params=limit(8),
         cost_estimate=pl.CostEstimate(flops=12 * UNITS * 24 * rank * rank, bytes_accessed=2**20, transcendentals=0),
@@ -463,47 +461,68 @@
     )(table, keep, *got, *([first] if joined else []))
 
 
-def pack_kernel(s0, s1, s2, s3, out_ref):
-    for m, ref in enumerate((s0, s1, s2, s3)):
-        out_ref[m] = ref[1]
-
-
-def pack(slots):
+def pack_kernel(own_ref, got_ref, *outs):
+    for m, ref in enumerate(outs):
+        ref[0] = own_ref[m]
+        ref[1] = got_ref[m]
+
+
+def pack(own, got):
     vmem = pl.BlockSpec(memory_space=pltpu.VMEM)
     return pl.pallas_call(
         pack_kernel,
-        in_specs=[vmem] * 4,
-        out_specs=vmem,
-        out_shape=jax.ShapeDtypeStruct((4,) + slots[0].shape[1:], F32),
+        in_specs=[vmem] * 2,
+        out_specs=[vmem] * 4,
+        out_shape=[jax.ShapeDtypeStruct((2,) + own.shape[1:], F32)] * 4,
         compiler_params=limit(4),
         cost_estimate=pl.CostEstimate(flops=0, bytes_accessed=2**19, transcendentals=0),
         name="pack",
-    )(*slots)
-
-
-def arrange_kernel(rank, table_ref, s0, s1, s2, s3, other_ref, out_ref, units):
+    )(own, got)
+
+
+def arrange_kernel(table_ref, s0, s1, s2, s3, out_ref, units):
+    rank = out_ref.shape[1] // 6
     for m, ref in enumerate((s0, s1, s2, s3)):
         units[4 * m : 4 * m + 4] = ref[0]
-        units[16 + 4 * m : 20 + 4 * m] = other_ref[m]
-    for v in range(0, 27):
+        units[16 + 4 * m : 20 + 4 * m] = ref[1]
+    for v in range(27):
         a, b, c = three(units[table_ref[FINAL + v]])
         for i, part in enumerate((a, a, b, a, b, c)):
             out_ref[24 * v : 24 * v + 24, rank * i : rank * (i + 1)] = part.astype(BF16)
 
 
-def arrange(table, slots, other):
-    rank = other.shape[-1]
-    vmem = pl.BlockSpec(memory_space=pltpu.VMEM)
-    return pl.pallas_call(
-        functools.partial(arrange_kernel, rank),
-        in_specs=[pl.BlockSpec(memory_space=pltpu.SMEM)] + [vmem] * 5,
+def arrange(table, slots):
+    rank = slots[0].shape[-1]
+    vmem = pl.BlockSpec(memory_space=pltpu.VMEM)
+    return pl.pallas_call(
+        arrange_kernel,
+        in_specs=[pl.BlockSpec(memory_space=pltpu.SMEM)] + [vmem] * 4,
         out_specs=vmem,
         out_shape=jax.ShapeDtypeStruct((27 * 24, 6 * rank), BF16),
         scratch_shapes=[pltpu.VMEM((32, 24, rank), F32)],
         compiler_params=limit(6),
         cost_estimate=pl.CostEstimate(flops=0, bytes_accessed=2**21, transcendentals=0),
         name="arrange",
-    )(table, *slots, other)
+    )(table, *slots)
+
+
+def final_kernel(scale, factor_ref, first_ref, second_ref, out_ref):
+    for i, ref in enumerate((first_ref, second_ref)):
+        made = lax.dot_general(ref[...], factor_ref[i], (((1,), (1,)), ((), ())), preferred_element_type=F32)
+        out_ref[i] = made * scale
+
+
+def final(factors, first, second, scale):
+    vmem = pl.BlockSpec(memory_space=pltpu.VMEM)
+    return pl.pallas_call(
+        functools.partial(final_kernel, scale),
+        in_specs=[vmem] * 3,
+        out_specs=vmem,
+        out_shape=jax.ShapeDtypeStruct((2, first.shape[0], first.shape[1] // 6), F32),
+        compiler_params=limit(6),
+        cost_estimate=pl.CostEstimate(flops=2**29, bytes_accessed=2**22, transcendentals=0),
+        name="final",
+    )(factors, first, second)
 
 
 def planes(activations, out_grads, omega):
@@ -541,17 +560,19 @@
         keep, *out = plane(table, act, got, own, other)
         got = move_all(out, z_masks)
         made = gather(table, keep, got, gram)
-        gram, slots = (made[0], list(made[1:])) if layer == 0 else (made[:2], list(made[2:]))
+        gram, (near, far) = made[:-2], made[-2:]
+        slots = list(pack(near, move(far, core_mask)))
         slots = slots[:1] + move_all(slots[1:], chip_masks)
-        other = move(pack(slots), core_mask)
-        held.append(arrange(table, slots, other))
+        gram = gram[0] if layer == 0 else gram
+        held.append(arrange(table, slots))
 
     mine = gram[0] + move(gram[1], core_mask)
     for masks in (z_masks, chip_masks):
         one, two, both = move_all([mine] * 3, masks)
         mine = (mine + one) + (two + both)
     theirs = move(mine, core_mask)
-    return finish(table, mine, theirs, *held, math.sqrt(27 * channels))
+    factors = inverses_of_factors(table, mine, theirs)
+    return final(factors, *held, math.sqrt(27 * channels))
 
 
 def solution(mesh):

time: 122 us -> 124 us (1.016)
  waiting for transfers between devices: 39.4 us -> 42.2 us
    ppermute x43, waiting for transfers between devices: 39.4 us -> 42.2 us  [swap(): return lax.ppermute(value, AXES, [(d, d ^ mask) for d in range(total)])]
    pallas_call x5 -> x6, Pallas kernels: 8.98 us -> 9.03 us  [the longest x1 6.09 us: inverses_of_factors(): pl.pallas_call(functools.partial(inverses_kernel, size), in_specs=[pl.Blo...]
  transfers between devices with their start and end apart: 44 -> 44, of which waited for: 15 -> 14; matrix products, arithmetic and copies ran while one was open for 2% -> 2% of each run, Pallas kernels for 16% -> 20%
where the time goes in v2:
time: 124 us
  starting transfers between devices  49.5 us (40%)
  waiting for transfers between devices  42.2 us (34%)
  Pallas kernels  28.2 us (23%)
  local copies, waits for them, and re-layouts  1.63 us (1%)
  matrix products  1.5 us (1%)
    ppermute x43, starting transfers between devices, swap(): return lax.ppermute(value, AXES, [(d, d ^ mask) for d in range(total)])  48.8 us
    ppermute x43, waiting for transfers between devices, swap(): return lax.ppermute(value, AXES, [(d, d ^ mask) for d in range(total)])  42.2 us
    pallas_call x2, Pallas kernels, plane(): pl.pallas_call(functools.partial(plane_kernel, frames, widths, rank), in_...  13.4 us
    pallas_call x1, Pallas kernels, inverses_of_factors(): pl.pallas_call(functools.partial(inverses_kernel, size), in_specs=[pl.Blo...  6.09 us
    pallas_call x2, Pallas kernels, turn(): pl.pallas_call(functools.partial(turn_kernel, frames, positions // frames...  2.94 us
  transfers between devices with their start and end apart: 44, of which 14 were waited for; matrix products, arithmetic and copies ran while one was open for 2% of the time, Pallas kernels for 20%

profile of v2, /device:TPU:0, one launch (start us, length us, event | category | flops | bytes accessed | tf_op | source)
XLA Modules:
  0.0 123.9 jit_solution(4758394791345483809)
XLA Ops:
  0.0 0.5 collective-permute-start
  0.5 0.9 copy-done
  1.4 1.5 %convolution_convert_fusion = bf16[1024,128]{1,0:T(8,128)(2,1)S(1)} fusion(bf16[1024,768]{1,0:T(8,128)(2,1)S(1)} %bitcast.19, bf16[768,128]{1,0:T(8,128)(2,1)} %param.6), kind=kOutput, calls=%fused_computation | convolution fusion | flops 201457664 | bytes 2031616 | tf_op jit(solution)/shard_map/dot_general | solution.py:547
  2.9 0.7 fusion.1
  3.6 0.7 collective-permute-start.4
  4.3 0.7 constant_dynamic-slice_fusion
  5.0 0.6 pieces.1
  5.6 9.9 %collective-permute-start.18 = (bf16[8,3,32,128]{3,2,1,0:T(8,128)(2,1)S(1)}, bf16[8,3,32,128]{3,2,1,0:T(8,128)(2,1)S(1)}, u32[]{:S(2)}, u32[]{:S(2)}) collective-permute-start(bf16[8,3,32,128]{3,2,1,0:T(8,128)(2,1)S(1)} %get-tuple-element.51.refs_4_), channel_id=1, source_target_pairs={{0,1},{1,0},{2,3},{3,2},{4,5},{5,4},{6,7},{7,6},{8,9},{9,8},{10,11... | collective-permute-start | bytes 589832 | tf_op jit(solution)/shard_map/ppermute | solution.py:19
  15.4 1.5 %collective-permute-start.19 = (bf16[8,3,32,128]{3,2,1,0:T(8,128)(2,1)S(1)}, bf16[8,3,32,128]{3,2,1,0:T(8,128)(2,1)S(1)}, u32[]{:S(2)}, u32[]{:S(2)}) collective-permute-start(bf16[8,3,32,128]{3,2,1,0:T(8,128)(2,1)S(1)} %get-tuple-element.51.refs_4_), channel_id=1, source_target_pairs={{0,16},{1,17},{2,18},{3,19},{4,20},{5,21},{6,22},{7,23},{8,24},{9,... | collective-permute-start | bytes 589832 | tf_op jit(solution)/shard_map/ppermute | solution.py:19
  17.0 0.0 collective-permute-start.20
  17.0 4.1 %collective-permute-done.18.refs_5_ = bf16[8,3,32,128]{3,2,1,0:T(8,128)(2,1)S(1)} collective-permute-done((bf16[8,3,32,128]{3,2,1,0:T(8,128)(2,1)S(1)}, bf16[8,3,32,128]{3,2,1,0:T(8,128)(2,1)S(1)}, u32[]{:S(2)}, u32[]{:S(2)}) %collective-permute-start.18) | collective-permute-done | bytes 196640 | tf_op jit(solution)/shard_map/ppermute | solution.py:19
  21.0 1.5 %collective-permute-start.6 = (bf16[8,3,32,128]{3,2,1,0:T(8,128)(2,1)S(1)}, bf16[8,3,32,128]{3,2,1,0:T(8,128)(2,1)S(1)}, u32[]{:S(2)}, u32[]{:S(2)}) collective-permute-start(bf16[8,3,32,128]{3,2,1,0:T(8,128)(2,1)S(1)} %get-tuple-element.42.refs_4_), channel_id=1, source_target_pairs={{0,16},{1,17},{2,18},{3,19},{4,20},{5,21},{6,22},{7,23},{8,24},{9,... | collective-permute-start | bytes 589832 | tf_op jit(solution)/shard_map/ppermute | solution.py:19
  22.6 6.2 %collective-permute-done.19.refs_6_ = bf16[8,3,32,128]{3,2,1,0:T(8,128)(2,1)S(1)} collective-permute-done((bf16[8,3,32,128]{3,2,1,0:T(8,128)(2,1)S(1)}, bf16[8,3,32,128]{3,2,1,0:T(8,128)(2,1)S(1)}, u32[]{:S(2)}, u32[]{:S(2)}) %collective-permute-start.19) | collective-permute-done | bytes 196640 | tf_op jit(solution)/shard_map/ppermute | solution.py:19
  28.7 0.5 collective-permute-start.7
  29.3 2.7 %collective-permute-start.5 = (bf16[8,3,32,128]{3,2,1,0:T(8,128)(2,1)S(1)}, bf16[8,3,32,128]{3,2,1,0:T(8,128)(2,1)S(1)}, u32[]{:S(2)}, u32[]{:S(2)}) collective-permute-start(bf16[8,3,32,128]{3,2,1,0:T(8,128)(2,1)S(1)} %get-tuple-element.42.refs_4_), channel_id=1, source_target_pairs={{0,1},{1,0},{2,3},{3,2},{4,5},{5,4},{6,7},{7,6},{8,9},{9,8},{10,11... | collective-permute-start | bytes 589832 | tf_op jit(solution)/shard_map/ppermute | solution.py:19
  32.0 0.5 collective-permute-start.22
  32.5 0.1 collective-permute-start.23
  32.5 1.5 %turn.3 = (bf16[96,1024]{1,0:T(8,128)(2,1)S(1)}, bf16[96,1024]{1,0:T(8,128)(2,1)S(1)}, bf16[96,1024]{1,0:T(8,128)(2,1)S(1)}, bf16[96,1024]{1,0:T(8,128)(2,1)S(1)}) custom-call(s32[174]{0:T(256)S(1)} %bitcast.27, bf16[2,512,768]{2,1,0:T(8,128)(2,1)S(1)} %bitcast.21, bf16[2,512,768]{2,1,0:T(8,128)(2,1)} %collective-permute-done.got_ref), custom_call_target="tpu_custom_call" | custom-call | bytes 1572864 | tf_op jit(solution)/shard_map/turn/pallas_call | solution.py:303
  34.0 1.3 %collective-permute-done.7.refs_7_ = bf16[8,3,32,128]{3,2,1,0:T(8,128)(2,1)S(1)} collective-permute-done((bf16[8,3,32,128]{3,2,1,0:T(8,128)(2,1)S(1)}, bf16[8,3,32,128]{3,2,1,0:T(8,128)(2,1)S(1)}, u32[]{:S(2)}, u32[]{:S(2)}) %collective-permute-start.7) | collective-permute-done | bytes 196640 | tf_op jit(solution)/shard_map/ppermute | solution.py:19
  35.3 2.4 %collective-permute-done.5.refs_5_ = bf16[8,3,32,128]{3,2,1,0:T(8,128)(2,1)S(1)} collective-permute-done((bf16[8,3,32,128]{3,2,1,0:T(8,128)(2,1)S(1)}, bf16[8,3,32,128]{3,2,1,0:T(8,128)(2,1)S(1)}, u32[]{:S(2)}, u32[]{:S(2)}) %collective-permute-start.5) | collective-permute-done | bytes 196640 | tf_op jit(solution)/shard_map/ppermute | solution.py:19
  37.7 0.6 collective-permute-start.16
  38.3 2.9 %collective-permute-start.17 = (bf16[96,1024]{1,0:T(8,128)(2,1)S(1)}, bf16[96,1024]{1,0:T(8,128)(2,1)S(1)}, u32[]{:S(2)}, u32[]{:S(2)}) collective-permute-start(bf16[96,1024]{1,0:T(8,128)(2,1)S(1)} %get-tuple-element.50), channel_id=1, source_target_pairs={{0,17},{1,16},{2,19},{3,18},{4,21},{5,20},{6,23},{7,22},{8,25},{9,... | collective-permute-start | bytes 589832 | tf_op jit(solution)/shard_map/ppermute | solution.py:19
  41.2 1.5 %turn.2 = (bf16[96,1024]{1,0:T(8,128)(2,1)S(1)}, bf16[96,1024]{1,0:T(8,128)(2,1)S(1)}, bf16[96,1024]{1,0:T(8,128)(2,1)S(1)}, bf16[96,1024]{1,0:T(8,128)(2,1)S(1)}) custom-call(s32[174]{0:T(256)S(1)} %bitcast.28, bf16[2,512,768]{2,1,0:T(8,128)(2,1)S(1)} %bitcast.22, bf16[2,512,768]{2,1,0:T(8,128)(2,1)} %collective-permute-done.got_ref), custom_call_target="tpu_custom_call" | custom-call | bytes 1572864 | tf_op jit(solution)/shard_map/turn/pallas_call | solution.py:303
  42.7 0.1 collective-permute-start.11
  42.8 0.5 collective-permute-start.9
  43.3 2.2 %collective-permute-done.15.refs_1_ = bf16[96,1024]{1,0:T(8,128)(2,1)S(1)} collective-permute-done((bf16[96,1024]{1,0:T(8,128)(2,1)S(1)}, bf16[96,1024]{1,0:T(8,128)(2,1)S(1)}, u32[]{:S(2)}, u32[]{:S(2)}) %collective-permute-start.15) | collective-permute-done | bytes 196640 | tf_op jit(solution)/shard_map/ppermute | solution.py:19
  45.5 4.1 %collective-permute-done.16.refs_2_ = bf16[96,1024]{1,0:T(8,128)(2,1)S(1)} collective-permute-done((bf16[96,1024]{1,0:T(8,128)(2,1)S(1)}, bf16[96,1024]{1,0:T(8,128)(2,1)S(1)}, u32[]{:S(2)}, u32[]{:S(2)}) %collective-permute-start.16) | collective-permute-done | bytes 196640 | tf_op jit(solution)/shard_map/ppermute | solution.py:19
  49.6 2.9 %collective-permute-start.3 = (bf16[96,1024]{1,0:T(8,128)(2,1)S(1)}, bf16[96,1024]{1,0:T(8,128)(2,1)S(1)}, u32[]{:S(2)}, u32[]{:S(2)}) collective-permute-start(bf16[96,1024]{1,0:T(8,128)(2,1)S(1)} %get-tuple-element.41), channel_id=1, source_target_pairs={{0,17},{1,16},{2,19},{3,18},{4,21},{5,20},{6,23},{7,22},{8,25},{9,... | collective-permute-start | bytes 589832 | tf_op jit(solution)/shard_map/ppermute | solution.py:19
  52.4 6.8 %plane.3 = (f32[28,24,128]{2,1,0:T(8,128)S(1)}, bf16[28,24,128]{2,1,0:T(8,128)(2,1)S(1)}, bf16[28,24,128]{2,1,0:T(8,128)(2,1)S(1)}, bf16[28,24,128]{2,1,0:T(8,128)(2,1)S(1)}) custom-call(s32[174]{0:T(256)S(1)} %bitcast.29, bf16[96,1024]{1,0:T(8,128)(2,1)S(1)} %get-tuple-element.47.refs_0_, bf16[96,1024]{1,0:T(8,128)(2,1)S(1)} %collective-permute-done.15.refs_1_, ...), custom_call_target="tpu_custom_call" | custom-call | flops 2717908992 | bytes 6291456 | tf_op jit(solution)/shard_map/plane/pallas_call | solution.py:394
  59.2 1.6 %collective-permute-start.25 = (bf16[28,24,128]{2,1,0:T(8,128)(2,1)S(1)}, bf16[28,24,128]{2,1,0:T(8,128)(2,1)S(1)}, u32[]{:S(2)}, u32[]{:S(2)}) collective-permute-start(bf16[28,24,128]{2,1,0:T(8,128)(2,1)S(1)} %get-tuple-element.53), channel_id=1, source_target_pairs={{0,2},{1,3},{2,0},{3,1},{4,6},{5,7},{6,4},{7,5},{8,10},{9,11},{10,... | collective-permute-start | bytes 516104 | tf_op jit(solution)/shard_map/ppermute | solution.py:19
  60.9 1.7 %collective-permute-start.26 = (bf16[28,24,128]{2,1,0:T(8,128)(2,1)S(1)}, bf16[28,24,128]{2,1,0:T(8,128)(2,1)S(1)}, u32[]{:S(2)}, u32[]{:S(2)}) collective-permute-start(bf16[28,24,128]{2,1,0:T(8,128)(2,1)S(1)} %get-tuple-element.54), channel_id=1, source_target_pairs={{0,4},{1,5},{2,6},{3,7},{4,0},{5,1},{6,2},{7,3},{8,12},{9,13},{10,... | collective-permute-start | bytes 516104 | tf_op jit(solution)/shard_map/ppermute | solution.py:19
  62.6 1.1 collective-permute-start.27
  63.7 6.6 %plane.2 = (f32[28,24,128]{2,1,0:T(8,128)S(1)}, bf16[28,24,128]{2,1,0:T(8,128)(2,1)S(1)}, bf16[28,24,128]{2,1,0:T(8,128)(2,1)S(1)}, bf16[28,24,128]{2,1,0:T(8,128)(2,1)S(1)}) custom-call(s32[174]{0:T(256)S(1)} %bitcast.30, bf16[96,1024]{1,0:T(8,128)(2,1)S(1)} %get-tuple-element.38.refs_0_, bf16[96,1024]{1,0:T(8,128)(2,1)S(1)} %collective-permute-done.1.refs_1_, ...), custom_call_target="tpu_custom_call" | custom-call | flops 2717908992 | bytes 6291456 | tf_op jit(solution)/shard_map/plane/pallas_call | solution.py:394
  70.3 0.7 collective-permute-start.12
  71.0 2.6 %collective-permute-start.13 = (bf16[28,24,128]{2,1,0:T(8,128)(2,1)S(1)}, bf16[28,24,128]{2,1,0:T(8,128)(2,1)S(1)}, u32[]{:S(2)}, u32[]{:S(2)}) collective-permute-start(bf16[28,24,128]{2,1,0:T(8,128)(2,1)S(1)} %get-tuple-element.45), channel_id=1, source_target_pairs={{0,4},{1,5},{2,6},{3,7},{4,0},{5,1},{6,2},{7,3},{8,12},{9,13},{10,... | collective-permute-start | bytes 516104 | tf_op jit(solution)/shard_map/ppermute | solution.py:19
  73.7 1.1 collective-permute-start.14
  74.8 1.2 collective-permute-done.26.refs_2_
  76.0 1.1 gather.2
  77.1 1.4 %collective-permute-done.12.refs_1_ = bf16[28,24,128]{2,1,0:T(8,128)(2,1)S(1)} collective-permute-done((bf16[28,24,128]{2,1,0:T(8,128)(2,1)S(1)}, bf16[28,24,128]{2,1,0:T(8,128)(2,1)S(1)}, u32[]{:S(2)}, u32[]{:S(2)}) %collective-permute-start.12) | collective-permute-done | bytes 172064 | tf_op jit(solution)/shard_map/ppermute | solution.py:19
  78.5 12.1 %collective-permute-done.13.refs_2_ = bf16[28,24,128]{2,1,0:T(8,128)(2,1)S(1)} collective-permute-done((bf16[28,24,128]{2,1,0:T(8,128)(2,1)S(1)}, bf16[28,24,128]{2,1,0:T(8,128)(2,1)S(1)}, u32[]{:S(2)}, u32[]{:S(2)}) %collective-permute-start.13) | collective-permute-done | bytes 172064 | tf_op jit(solution)/shard_map/ppermute | solution.py:19
  90.6 1.1 gather.3
  91.7 0.1 collective-permute-start.28
  91.8 1.2 collective-permute-done.28
  93.0 2.4 %collective-permute-start.29 = (f32[72,128]{1,0:T(8,128)S(1)}, f32[72,128]{1,0:T(8,128)S(1)}, u32[]{:S(2)}, u32[]{:S(2)}) collective-permute-start(f32[72,128]{1,0:T(8,128)S(1)} %add.30), channel_id=1, source_target_pairs={{0,2},{1,3},{2,0},{3,1},{4,6},{5,7},{6,4},{7,5},{8,10},{9,11},{10,... | collective-permute-start | bytes 110600 | tf_op jit(solution)/shard_map/ppermute | solution.py:19
  95.4 1.0 collective-permute-start.30
  96.5 1.4 %collective-permute-start.31 = (f32[72,128]{1,0:T(8,128)S(1)}, f32[72,128]{1,0:T(8,128)S(1)}, u32[]{:S(2)}, u32[]{:S(2)}) collective-permute-start(f32[72,128]{1,0:T(8,128)S(1)} %add.30), channel_id=1, source_target_pairs={{0,6},{1,7},{2,4},{3,5},{4,2},{5,3},{6,0},{7,1},{8,14},{9,15},{10,... | collective-permute-start | bytes 110600 | tf_op jit(solution)/shard_map/ppermute | solution.py:19
  97.9 3.5 %collective-permute-done.30 = f32[72,128]{1,0:T(8,128)S(1)} collective-permute-done((f32[72,128]{1,0:T(8,128)S(1)}, f32[72,128]{1,0:T(8,128)S(1)}, u32[]{:S(2)}, u32[]{:S(2)}) %collective-permute-start.30) | collective-permute-done | bytes 36896 | tf_op jit(solution)/shard_map/ppermute | solution.py:19
  101.4 0.9 collective-permute-done.31
  102.2 0.6 collective-permute-start.32
  102.8 0.4 collective-permute-start.33
  103.2 2.6 %collective-permute-start.34 = (f32[72,128]{1,0:T(8,128)S(1)}, f32[72,128]{1,0:T(8,128)S(1)}, u32[]{:S(2)}, u32[]{:S(2)}) collective-permute-start(f32[72,128]{1,0:T(8,128)S(1)} %add_add_fusion.1), channel_id=1, source_target_pairs={{0,17},{1,16},{2,19},{3,18},{4,21},{5,20},{6,23},{7,22},{8,25},{9,... | collective-permute-start | bytes 110600 | tf_op jit(solution)/shard_map/ppermute | solution.py:19
  105.8 0.6 collective-permute-start.41
  106.4 0.4 collective-permute-done.33
  106.8 1.3 %collective-permute-done.34 = f32[72,128]{1,0:T(8,128)S(1)} collective-permute-done((f32[72,128]{1,0:T(8,128)S(1)}, f32[72,128]{1,0:T(8,128)S(1)}, u32[]{:S(2)}, u32[]{:S(2)}) %collective-permute-start.34) | collective-permute-done | bytes 36896 | tf_op jit(solution)/shard_map/ppermute | solution.py:19
  108.0 0.1 collective-permute-start.35
  108.1 1.7 %collective-permute-start.42 = (f32[2,4,24,128]{3,2,1,0:T(8,128)S(1)}, f32[2,4,24,128]{3,2,1,0:T(8,128)S(1)}, u32[]{:S(2)}, u32[]{:S(2)}) collective-permute-start(f32[2,4,24,128]{3,2,1,0:T(8,128)S(1)} %get-tuple-element.69), channel_id=1, source_target_pairs={{0,16},{1,17},{2,18},{3,19},{4,20},{5,21},{6,22},{7,23},{8,24},{9,... | collective-permute-start | bytes 294920 | tf_op jit(solution)/shard_map/ppermute | solution.py:19
  109.8 1.4 %collective-permute-start.43 = (f32[2,4,24,128]{3,2,1,0:T(8,128)S(1)}, f32[2,4,24,128]{3,2,1,0:T(8,128)S(1)}, u32[]{:S(2)}, u32[]{:S(2)}) collective-permute-start(f32[2,4,24,128]{3,2,1,0:T(8,128)S(1)} %get-tuple-element.70), channel_id=1, source_target_pairs={{0,17},{1,16},{2,19},{3,18},{4,21},{5,20},{6,23},{7,22},{8,25},{9,... | collective-permute-start | bytes 294920 | tf_op jit(solution)/shard_map/ppermute | solution.py:19
  111.3 0.5 collective-permute-start.37
  111.8 1.6 %collective-permute-start.38 = (f32[2,4,24,128]{3,2,1,0:T(8,128)S(1)}, f32[2,4,24,128]{3,2,1,0:T(8,128)S(1)}, u32[]{:S(2)}, u32[]{:S(2)}) collective-permute-start(f32[2,4,24,128]{3,2,1,0:T(8,128)S(1)} %get-tuple-element.63), channel_id=1, source_target_pairs={{0,16},{1,17},{2,18},{3,19},{4,20},{5,21},{6,22},{7,23},{8,24},{9,... | collective-permute-start | bytes 294920 | tf_op jit(solution)/shard_map/ppermute | solution.py:19
  113.4 1.4 %collective-permute-start.39 = (f32[2,4,24,128]{3,2,1,0:T(8,128)S(1)}, f32[2,4,24,128]{3,2,1,0:T(8,128)S(1)}, u32[]{:S(2)}, u32[]{:S(2)}) collective-permute-start(f32[2,4,24,128]{3,2,1,0:T(8,128)S(1)} %get-tuple-element.64), channel_id=1, source_target_pairs={{0,17},{1,16},{2,19},{3,18},{4,21},{5,20},{6,23},{7,22},{8,25},{9,... | collective-permute-start | bytes 294920 | tf_op jit(solution)/shard_map/ppermute | solution.py:19
  114.8 6.1 %inverses.1.factor_ref = bf16[2,128,768]{2,1,0:T(8,128)(2,1)S(1)} custom-call(s32[174]{0:T(256)S(1)} %bitcast.33, f32[72,128]{1,0:T(8,128)S(1)} %add_add_fusion.mine_ref, f32[72,128]{1,0:T(8,128)S(1)} %collective-permute-done.35.theirs_ref), custom_call_target="tpu_custom_call" | custom-call | flops 1073741824 | bytes 1048576 | tf_op jit(solution)/shard_map/inverses/pallas_call | solution.py:169
  121.0 0.7 arrange.3.second_ref
  121.7 0.7 arrange.2.first_ref
  122.4 1.5 %final.1 = f32[2,648,128]{2,1,0:T(8,128)} custom-call(bf16[2,128,768]{2,1,0:T(8,128)(2,1)S(1)} %inverses.1.factor_ref, bf16[648,768]{1,0:T(8,128)(2,1)S(1)} %arrange.2.first_ref, bf16[648,768]{1,0:T(8,128)(2,1)S(1)} %arrange.3.second_ref), custom_call_target="tpu_custom_call" | custom-call | flops 536870912 | bytes 4194304 | tf_op jit(solution)/shard_map/final/pallas_call | solution.py:517
  (47 shorter events, 0.2 us)
Async XLA Ops:
  0.0 1.4 %copy-start = (bf16[2,1,8,2,32,768]{5,4,3,2,1,0:T(8,128)(2,1)S(1)}, bf16[2,1,8,2,32,768]{5,4,3,2,1,0:T(8,128)(2,1)}, u32[]{:S(2)}) copy-start(bf16[2,1,8,2,32,768]{5,4,3,2,1,0:T(8,128)(2,1)} %param.5) | copy-start | bytes 4718596
  0.0 32.5 %copy-start.1 = (bf16[2,1,8,2,32,768]{5,4,3,2,1,0:T(8,128)(2,1)S(1)}, bf16[2,1,8,2,32,768]{5,4,3,2,1,0:T(8,128)(2,1)}, u32[]{:S(2)}) copy-start(bf16[2,1,8,2,32,768]{5,4,3,2,1,0:T(8,128)(2,1)} %param.4) | copy-start | bytes 4718596
  0.0 32.5 %collective-permute-start = (bf16[2,512,768]{2,1,0:T(8,128)(2,1)}, bf16[2,512,768]{2,1,0:T(8,128)(2,1)}, u32[]{:S(2)}, u32[]{:S(2)}) collective-permute-start(bf16[2,512,768]{2,1,0:T(8,128)(2,1)} %bitcast.20), channel_id=1, source_target_pairs={{0,8},{1,9},{2,10},{3,11},{4,12},{5,13},{6,14},{7,15},{8,0},{9,1},... | collective-permute-start | bytes 4718600 | tf_op jit(solution)/shard_map/ppermute | solution.py:19
  3.6 1.4 %collective-permute-start.4 = (bf16[2,8,32,128]{3,2,1,0:T(8,128)(2,1)}, bf16[2,8,32,128]{3,2,1,0:T(8,128)(2,1)S(1)}, u32[]{:S(2)}, u32[]{:S(2)}) collective-permute-start(bf16[2,8,32,128]{3,2,1,0:T(8,128)(2,1)} %fusion.1), channel_id=1, source_target_pairs={{1,2},{3,4},{5,6},{2,1},{4,3},{6,5},{9,10},{11,12},{13,14},{10,9},... | collective-permute-start | bytes 393224 | tf_op jit(solution)/shard_map/ppermute | solution.py:551
  5.6 15.5 %collective-permute-start.18 = (bf16[8,3,32,128]{3,2,1,0:T(8,128)(2,1)S(1)}, bf16[8,3,32,128]{3,2,1,0:T(8,128)(2,1)S(1)}, u32[]{:S(2)}, u32[]{:S(2)}) collective-permute-start(bf16[8,3,32,128]{3,2,1,0:T(8,128)(2,1)S(1)} %get-tuple-element.51.refs_4_), channel_id=1, source_target_pairs={{0,1},{1,0},{2,3},{3,2},{4,5},{5,4},{6,7},{7,6},{8,9},{9,8},{10,11... | collective-permute-start | bytes 589832 | tf_op jit(solution)/shard_map/ppermute | solution.py:19
  15.4 13.3 %collective-permute-start.19 = (bf16[8,3,32,128]{3,2,1,0:T(8,128)(2,1)S(1)}, bf16[8,3,32,128]{3,2,1,0:T(8,128)(2,1)S(1)}, u32[]{:S(2)}, u32[]{:S(2)}) collective-permute-start(bf16[8,3,32,128]{3,2,1,0:T(8,128)(2,1)S(1)} %get-tuple-element.51.refs_4_), channel_id=1, source_target_pairs={{0,16},{1,17},{2,18},{3,19},{4,20},{5,21},{6,22},{7,23},{8,24},{9,... | collective-permute-start | bytes 589832 | tf_op jit(solution)/shard_map/ppermute | solution.py:19
  17.0 12.3 %collective-permute-start.20 = (bf16[8,3,32,128]{3,2,1,0:T(8,128)(2,1)S(1)}, bf16[8,3,32,128]{3,2,1,0:T(8,128)(2,1)S(1)}, u32[]{:S(2)}, u32[]{:S(2)}) collective-permute-start(bf16[8,3,32,128]{3,2,1,0:T(8,128)(2,1)S(1)} %get-tuple-element.51.refs_4_), channel_id=1, source_target_pairs={{0,17},{1,16},{2,19},{3,18},{4,21},{5,20},{6,23},{7,22},{8,25},{9,... | collective-permute-start | bytes 589832 | tf_op jit(solution)/shard_map/ppermute | solution.py:19
  17.0 15.0 %collective-permute-start.21 = (bf16[8,3,32,128]{3,2,1,0:T(8,128)(2,1)S(1)}, bf16[8,3,32,128]{3,2,1,0:T(8,128)(2,1)S(1)}, u32[]{:S(2)}, u32[]{:S(2)}) collective-permute-start(bf16[8,3,32,128]{3,2,1,0:T(8,128)(2,1)S(1)} %get-tuple-element.51.refs_4_), channel_id=1, source_target_pairs={{0,8},{1,9},{2,10},{3,11},{4,12},{5,13},{6,14},{7,15},{8,0},{9,1},... | collective-permute-start | bytes 589832 | tf_op jit(solution)/shard_map/ppermute | solution.py:19
  21.0 10.9 %collective-permute-start.6 = (bf16[8,3,32,128]{3,2,1,0:T(8,128)(2,1)S(1)}, bf16[8,3,32,128]{3,2,1,0:T(8,128)(2,1)S(1)}, u32[]{:S(2)}, u32[]{:S(2)}) collective-permute-start(bf16[8,3,32,128]{3,2,1,0:T(8,128)(2,1)S(1)} %get-tuple-element.42.refs_4_), channel_id=1, source_target_pairs={{0,16},{1,17},{2,18},{3,19},{4,20},{5,21},{6,22},{7,23},{8,24},{9,... | collective-permute-start | bytes 589832 | tf_op jit(solution)/shard_map/ppermute | solution.py:19
  28.7 6.6 %collective-permute-start.7 = (bf16[8,3,32,128]{3,2,1,0:T(8,128)(2,1)S(1)}, bf16[8,3,32,128]{3,2,1,0:T(8,128)(2,1)S(1)}, u32[]{:S(2)}, u32[]{:S(2)}) collective-permute-start(bf16[8,3,32,128]{3,2,1,0:T(8,128)(2,1)S(1)} %get-tuple-element.42.refs_4_), channel_id=1, source_target_pairs={{0,17},{1,16},{2,19},{3,18},{4,21},{5,20},{6,23},{7,22},{8,25},{9,... | collective-permute-start | bytes 589832 | tf_op jit(solution)/shard_map/ppermute | solution.py:19
  29.3 8.4 %collective-permute-start.5 = (bf16[8,3,32,128]{3,2,1,0:T(8,128)(2,1)S(1)}, bf16[8,3,32,128]{3,2,1,0:T(8,128)(2,1)S(1)}, u32[]{:S(2)}, u32[]{:S(2)}) collective-permute-start(bf16[8,3,32,128]{3,2,1,0:T(8,128)(2,1)S(1)} %get-tuple-element.42.refs_4_), channel_id=1, source_target_pairs={{0,1},{1,0},{2,3},{3,2},{4,5},{5,4},{6,7},{7,6},{8,9},{9,8},{10,11... | collective-permute-start | bytes 589832 | tf_op jit(solution)/shard_map/ppermute | solution.py:19
  31.9 5.7 %collective-permute-start.8 = (bf16[8,3,32,128]{3,2,1,0:T(8,128)(2,1)S(1)}, bf16[8,3,32,128]{3,2,1,0:T(8,128)(2,1)S(1)}, u32[]{:S(2)}, u32[]{:S(2)}) collective-permute-start(bf16[8,3,32,128]{3,2,1,0:T(8,128)(2,1)S(1)} %get-tuple-element.42.refs_4_), channel_id=1, source_target_pairs={{0,8},{1,9},{2,10},{3,11},{4,12},{5,13},{6,14},{7,15},{8,0},{9,1},... | collective-permute-start | bytes 589832 | tf_op jit(solution)/shard_map/ppermute | solution.py:19
  32.0 5.8 %collective-permute-start.22 = (bf16[8,3,32,128]{3,2,1,0:T(8,128)(2,1)S(1)}, bf16[8,3,32,128]{3,2,1,0:T(8,128)(2,1)S(1)}, u32[]{:S(2)}, u32[]{:S(2)}) collective-permute-start(bf16[8,3,32,128]{3,2,1,0:T(8,128)(2,1)S(1)} %collective-permute-done.18.refs_5_), channel_id=1, source_target_pairs={{0,8},{1,9},{2,10},{3,11},{4,12},{5,13},{6,14},{7,15},{8,0},{9,1},... | collective-permute-start | bytes 589832 | tf_op jit(solution)/shard_map/ppermute | solution.py:19
  32.5 5.8 %collective-permute-start.23 = (bf16[8,3,32,128]{3,2,1,0:T(8,128)(2,1)S(1)}, bf16[8,3,32,128]{3,2,1,0:T(8,128)(2,1)S(1)}, u32[]{:S(2)}, u32[]{:S(2)}) collective-permute-start(bf16[8,3,32,128]{3,2,1,0:T(8,128)(2,1)S(1)} %collective-permute-done.19.refs_6_), channel_id=1, source_target_pairs={{0,8},{1,9},{2,10},{3,11},{4,12},{5,13},{6,14},{7,15},{8,0},{9,1},... | collective-permute-start | bytes 589832 | tf_op jit(solution)/shard_map/ppermute | solution.py:19
  35.3 7.4 %collective-permute-start.24 = (bf16[8,3,32,128]{3,2,1,0:T(8,128)(2,1)S(1)}, bf16[8,3,32,128]{3,2,1,0:T(8,128)(2,1)S(1)}, u32[]{:S(2)}, u32[]{:S(2)}) collective-permute-start(bf16[8,3,32,128]{3,2,1,0:T(8,128)(2,1)S(1)} %collective-permute-done.20.refs_7_), channel_id=1, source_target_pairs={{0,8},{1,9},{2,10},{3,11},{4,12},{5,13},{6,14},{7,15},{8,0},{9,1},... | collective-permute-start | bytes 589832 | tf_op jit(solution)/shard_map/ppermute | solution.py:19
  37.7 5.1 %collective-permute-start.10 = (bf16[8,3,32,128]{3,2,1,0:T(8,128)(2,1)S(1)}, bf16[8,3,32,128]{3,2,1,0:T(8,128)(2,1)S(1)}, u32[]{:S(2)}, u32[]{:S(2)}) collective-permute-start(bf16[8,3,32,128]{3,2,1,0:T(8,128)(2,1)S(1)} %collective-permute-done.6.refs_6_), channel_id=1, source_target_pairs={{0,8},{1,9},{2,10},{3,11},{4,12},{5,13},{6,14},{7,15},{8,0},{9,1},... | collective-permute-start | bytes 589832 | tf_op jit(solution)/shard_map/ppermute | solution.py:19
  37.7 7.8 %collective-permute-start.15 = (bf16[96,1024]{1,0:T(8,128)(2,1)S(1)}, bf16[96,1024]{1,0:T(8,128)(2,1)S(1)}, u32[]{:S(2)}, u32[]{:S(2)}) collective-permute-start(bf16[96,1024]{1,0:T(8,128)(2,1)S(1)} %get-tuple-element.48), channel_id=1, source_target_pairs={{0,1},{1,0},{2,3},{3,2},{4,5},{5,4},{6,7},{7,6},{8,9},{9,8},{10,11... | collective-permute-start | bytes 589832 | tf_op jit(solution)/shard_map/ppermute | solution.py:19
  37.7 11.8 %collective-permute-start.16 = (bf16[96,1024]{1,0:T(8,128)(2,1)S(1)}, bf16[96,1024]{1,0:T(8,128)(2,1)S(1)}, u32[]{:S(2)}, u32[]{:S(2)}) collective-permute-start(bf16[96,1024]{1,0:T(8,128)(2,1)S(1)} %get-tuple-element.49), channel_id=1, source_target_pairs={{0,16},{1,17},{2,18},{3,19},{4,20},{5,21},{6,22},{7,23},{8,24},{9,... | collective-permute-start | bytes 589832 | tf_op jit(solution)/shard_map/ppermute | solution.py:19
  38.3 11.3 %collective-permute-start.17 = (bf16[96,1024]{1,0:T(8,128)(2,1)S(1)}, bf16[96,1024]{1,0:T(8,128)(2,1)S(1)}, u32[]{:S(2)}, u32[]{:S(2)}) collective-permute-start(bf16[96,1024]{1,0:T(8,128)(2,1)S(1)} %get-tuple-element.50), channel_id=1, source_target_pairs={{0,17},{1,16},{2,19},{3,18},{4,21},{5,20},{6,23},{7,22},{8,25},{9,... | collective-permute-start | bytes 589832 | tf_op jit(solution)/shard_map/ppermute | solution.py:19
  42.7 16.5 %collective-permute-start.11 = (bf16[8,3,32,128]{3,2,1,0:T(8,128)(2,1)S(1)}, bf16[8,3,32,128]{3,2,1,0:T(8,128)(2,1)S(1)}, u32[]{:S(2)}, u32[]{:S(2)}) collective-permute-start(bf16[8,3,32,128]{3,2,1,0:T(8,128)(2,1)S(1)} %collective-permute-done.7.refs_7_), channel_id=1, source_target_pairs={{0,8},{1,9},{2,10},{3,11},{4,12},{5,13},{6,14},{7,15},{8,0},{9,1},... | collective-permute-start | bytes 589832 | tf_op jit(solution)/shard_map/ppermute | solution.py:19
  42.8 18.1 %collective-permute-start.9 = (bf16[8,3,32,128]{3,2,1,0:T(8,128)(2,1)S(1)}, bf16[8,3,32,128]{3,2,1,0:T(8,128)(2,1)S(1)}, u32[]{:S(2)}, u32[]{:S(2)}) collective-permute-start(bf16[8,3,32,128]{3,2,1,0:T(8,128)(2,1)S(1)} %collective-permute-done.5.refs_5_), channel_id=1, source_target_pairs={{0,8},{1,9},{2,10},{3,11},{4,12},{5,13},{6,14},{7,15},{8,0},{9,1},... | collective-permute-start | bytes 589832 | tf_op jit(solution)/shard_map/ppermute | solution.py:19
  45.5 17.1 %collective-permute-start.1 = (bf16[96,1024]{1,0:T(8,128)(2,1)S(1)}, bf16[96,1024]{1,0:T(8,128)(2,1)S(1)}, u32[]{:S(2)}, u32[]{:S(2)}) collective-permute-start(bf16[96,1024]{1,0:T(8,128)(2,1)S(1)} %get-tuple-element.39), channel_id=1, source_target_pairs={{0,1},{1,0},{2,3},{3,2},{4,5},{5,4},{6,7},{7,6},{8,9},{9,8},{10,11... | collective-permute-start | bytes 589832 | tf_op jit(solution)/shard_map/ppermute | solution.py:19
  49.6 14.1 %collective-permute-start.2 = (bf16[96,1024]{1,0:T(8,128)(2,1)S(1)}, bf16[96,1024]{1,0:T(8,128)(2,1)S(1)}, u32[]{:S(2)}, u32[]{:S(2)}) collective-permute-start(bf16[96,1024]{1,0:T(8,128)(2,1)S(1)} %get-tuple-element.40), channel_id=1, source_target_pairs={{0,16},{1,17},{2,18},{3,19},{4,20},{5,21},{6,22},{7,23},{8,24},{9,... | collective-permute-start | bytes 589832 | tf_op jit(solution)/shard_map/ppermute | solution.py:19
  49.6 14.1 %collective-permute-start.3 = (bf16[96,1024]{1,0:T(8,128)(2,1)S(1)}, bf16[96,1024]{1,0:T(8,128)(2,1)S(1)}, u32[]{:S(2)}, u32[]{:S(2)}) collective-permute-start(bf16[96,1024]{1,0:T(8,128)(2,1)S(1)} %get-tuple-element.41), channel_id=1, source_target_pairs={{0,17},{1,16},{2,19},{3,18},{4,21},{5,20},{6,23},{7,22},{8,25},{9,... | collective-permute-start | bytes 589832 | tf_op jit(solution)/shard_map/ppermute | solution.py:19
  59.2 14.4 %collective-permute-start.25 = (bf16[28,24,128]{2,1,0:T(8,128)(2,1)S(1)}, bf16[28,24,128]{2,1,0:T(8,128)(2,1)S(1)}, u32[]{:S(2)}, u32[]{:S(2)}) collective-permute-start(bf16[28,24,128]{2,1,0:T(8,128)(2,1)S(1)} %get-tuple-element.53), channel_id=1, source_target_pairs={{0,2},{1,3},{2,0},{3,1},{4,6},{5,7},{6,4},{7,5},{8,10},{9,11},{10,... | collective-permute-start | bytes 516104 | tf_op jit(solution)/shard_map/ppermute | solution.py:19
  60.9 15.1 %collective-permute-start.26 = (bf16[28,24,128]{2,1,0:T(8,128)(2,1)S(1)}, bf16[28,24,128]{2,1,0:T(8,128)(2,1)S(1)}, u32[]{:S(2)}, u32[]{:S(2)}) collective-permute-start(bf16[28,24,128]{2,1,0:T(8,128)(2,1)S(1)} %get-tuple-element.54), channel_id=1, source_target_pairs={{0,4},{1,5},{2,6},{3,7},{4,0},{5,1},{6,2},{7,3},{8,12},{9,13},{10,... | collective-permute-start | bytes 516104 | tf_op jit(solution)/shard_map/ppermute | solution.py:19
  62.6 13.4 %collective-permute-start.27 = (bf16[28,24,128]{2,1,0:T(8,128)(2,1)S(1)}, bf16[28,24,128]{2,1,0:T(8,128)(2,1)S(1)}, u32[]{:S(2)}, u32[]{:S(2)}) collective-permute-start(bf16[28,24,128]{2,1,0:T(8,128)(2,1)S(1)} %get-tuple-element.55), channel_id=1, source_target_pairs={{0,6},{1,7},{2,4},{3,5},{4,2},{5,3},{6,0},{7,1},{8,14},{9,15},{10,... | collective-permute-start | bytes 516104 | tf_op jit(solution)/shard_map/ppermute | solution.py:19
  70.3 8.2 %collective-permute-start.12 = (bf16[28,24,128]{2,1,0:T(8,128)(2,1)S(1)}, bf16[28,24,128]{2,1,0:T(8,128)(2,1)S(1)}, u32[]{:S(2)}, u32[]{:S(2)}) collective-permute-start(bf16[28,24,128]{2,1,0:T(8,128)(2,1)S(1)} %get-tuple-element.44), channel_id=1, source_target_pairs={{0,2},{1,3},{2,0},{3,1},{4,6},{5,7},{6,4},{7,5},{8,10},{9,11},{10,... | collective-permute-start | bytes 516104 | tf_op jit(solution)/shard_map/ppermute | solution.py:19
  71.0 19.6 %collective-permute-start.13 = (bf16[28,24,128]{2,1,0:T(8,128)(2,1)S(1)}, bf16[28,24,128]{2,1,0:T(8,128)(2,1)S(1)}, u32[]{:S(2)}, u32[]{:S(2)}) collective-permute-start(bf16[28,24,128]{2,1,0:T(8,128)(2,1)S(1)} %get-tuple-element.45), channel_id=1, source_target_pairs={{0,4},{1,5},{2,6},{3,7},{4,0},{5,1},{6,2},{7,3},{8,12},{9,13},{10,... | collective-permute-start | bytes 516104 | tf_op jit(solution)/shard_map/ppermute | solution.py:19
  73.7 16.9 %collective-permute-start.14 = (bf16[28,24,128]{2,1,0:T(8,128)(2,1)S(1)}, bf16[28,24,128]{2,1,0:T(8,128)(2,1)S(1)}, u32[]{:S(2)}, u32[]{:S(2)}) collective-permute-start(bf16[28,24,128]{2,1,0:T(8,128)(2,1)S(1)} %get-tuple-element.46), channel_id=1, source_target_pairs={{0,6},{1,7},{2,4},{3,5},{4,2},{5,3},{6,0},{7,1},{8,14},{9,15},{10,... | collective-permute-start | bytes 516104 | tf_op jit(solution)/shard_map/ppermute | solution.py:19
  91.7 1.3 %collective-permute-start.28 = (f32[72,128]{1,0:T(8,128)S(1)}, f32[72,128]{1,0:T(8,128)S(1)}, u32[]{:S(2)}, u32[]{:S(2)}) collective-permute-start(f32[72,128]{1,0:T(8,128)S(1)} %get-tuple-element.58), channel_id=1, source_target_pairs={{0,8},{1,9},{2,10},{3,11},{4,12},{5,13},{6,14},{7,15},{8,0},{9,1},... | collective-permute-start | bytes 110600 | tf_op jit(solution)/shard_map/ppermute | solution.py:19
  93.0 4.8 %collective-permute-start.29 = (f32[72,128]{1,0:T(8,128)S(1)}, f32[72,128]{1,0:T(8,128)S(1)}, u32[]{:S(2)}, u32[]{:S(2)}) collective-permute-start(f32[72,128]{1,0:T(8,128)S(1)} %add.30), channel_id=1, source_target_pairs={{0,2},{1,3},{2,0},{3,1},{4,6},{5,7},{6,4},{7,5},{8,10},{9,11},{10,... | collective-permute-start | bytes 110600 | tf_op jit(solution)/shard_map/ppermute | solution.py:19
  95.4 5.9 %collective-permute-start.30 = (f32[72,128]{1,0:T(8,128)S(1)}, f32[72,128]{1,0:T(8,128)S(1)}, u32[]{:S(2)}, u32[]{:S(2)}) collective-permute-start(f32[72,128]{1,0:T(8,128)S(1)} %add.30), channel_id=1, source_target_pairs={{0,4},{1,5},{2,6},{3,7},{4,0},{5,1},{6,2},{7,3},{8,12},{9,13},{10,... | collective-permute-start | bytes 110600 | tf_op jit(solution)/shard_map/ppermute | solution.py:19
  96.5 5.8 %collective-permute-start.31 = (f32[72,128]{1,0:T(8,128)S(1)}, f32[72,128]{1,0:T(8,128)S(1)}, u32[]{:S(2)}, u32[]{:S(2)}) collective-permute-start(f32[72,128]{1,0:T(8,128)S(1)} %add.30), channel_id=1, source_target_pairs={{0,6},{1,7},{2,4},{3,5},{4,2},{5,3},{6,0},{7,1},{8,14},{9,15},{10,... | collective-permute-start | bytes 110600 | tf_op jit(solution)/shard_map/ppermute | solution.py:19
  97.9 7.9 %collective-permute-start.40 = (f32[4,4,24,128]{3,2,1,0:T(8,128)S(1)}, f32[4,4,24,128]{3,2,1,0:T(8,128)S(1)}, u32[]{:S(2)}, u32[]{:S(2)}) collective-permute-start(f32[4,4,24,128]{3,2,1,0:T(8,128)S(1)} %get-tuple-element.66), channel_id=1, source_target_pairs={{0,8},{1,9},{2,10},{3,11},{4,12},{5,13},{6,14},{7,15},{8,0},{9,1},... | collective-permute-start | bytes 589832 | tf_op jit(solution)/shard_map/ppermute | solution.py:19
  102.2 4.2 %collective-permute-start.32 = (f32[72,128]{1,0:T(8,128)S(1)}, f32[72,128]{1,0:T(8,128)S(1)}, u32[]{:S(2)}, u32[]{:S(2)}) collective-permute-start(f32[72,128]{1,0:T(8,128)S(1)} %add_add_fusion.1), channel_id=1, source_target_pairs={{0,1},{1,0},{2,3},{3,2},{4,5},{5,4},{6,7},{7,6},{8,9},{9,8},{10,11... | collective-permute-start | bytes 110600 | tf_op jit(solution)/shard_map/ppermute | solution.py:19
  102.8 4.0 %collective-permute-start.33 = (f32[72,128]{1,0:T(8,128)S(1)}, f32[72,128]{1,0:T(8,128)S(1)}, u32[]{:S(2)}, u32[]{:S(2)}) collective-permute-start(f32[72,128]{1,0:T(8,128)S(1)} %add_add_fusion.1), channel_id=1, source_target_pairs={{0,16},{1,17},{2,18},{3,19},{4,20},{5,21},{6,22},{7,23},{8,24},{9,... | collective-permute-start | bytes 110600 | tf_op jit(solution)/shard_map/ppermute | solution.py:19
  103.2 4.9 %collective-permute-start.34 = (f32[72,128]{1,0:T(8,128)S(1)}, f32[72,128]{1,0:T(8,128)S(1)}, u32[]{:S(2)}, u32[]{:S(2)}) collective-permute-start(f32[72,128]{1,0:T(8,128)S(1)} %add_add_fusion.1), channel_id=1, source_target_pairs={{0,17},{1,16},{2,19},{3,18},{4,21},{5,20},{6,23},{7,22},{8,25},{9,... | collective-permute-start | bytes 110600 | tf_op jit(solution)/shard_map/ppermute | solution.py:19
  105.8 5.5 %collective-permute-start.36 = (f32[4,4,24,128]{3,2,1,0:T(8,128)S(1)}, f32[4,4,24,128]{3,2,1,0:T(8,128)S(1)}, u32[]{:S(2)}, u32[]{:S(2)}) collective-permute-start(f32[4,4,24,128]{3,2,1,0:T(8,128)S(1)} %get-tuple-element.60), channel_id=1, source_target_pairs={{0,8},{1,9},{2,10},{3,11},{4,12},{5,13},{6,14},{7,15},{8,0},{9,1},... | collective-permute-start | bytes 589832 | tf_op jit(solution)/shard_map/ppermute | solution.py:19
  105.8 7.6 %collective-permute-start.41 = (f32[2,4,24,128]{3,2,1,0:T(8,128)S(1)}, f32[2,4,24,128]{3,2,1,0:T(8,128)S(1)}, u32[]{:S(2)}, u32[]{:S(2)}) collective-permute-start(f32[2,4,24,128]{3,2,1,0:T(8,128)S(1)} %get-tuple-element.68), channel_id=1, source_target_pairs={{0,1},{1,0},{2,3},{3,2},{4,5},{5,4},{6,7},{7,6},{8,9},{9,8},{10,11... | collective-permute-start | bytes 294920 | tf_op jit(solution)/shard_map/ppermute | solution.py:19
  108.0 3.7 %collective-permute-start.35 = (f32[72,128]{1,0:T(8,128)S(1)}, f32[72,128]{1,0:T(8,128)S(1)}, u32[]{:S(2)}, u32[]{:S(2)}) collective-permute-start(f32[72,128]{1,0:T(8,128)S(1)} %add_add_fusion.mine_ref), channel_id=1, source_target_pairs={{0,8},{1,9},{2,10},{3,11},{4,12},{5,13},{6,14},{7,15},{8,0},{9,1},... | collective-permute-start | bytes 110600 | tf_op jit(solution)/shard_map/ppermute | solution.py:19
  108.1 12.8 %collective-permute-start.42 = (f32[2,4,24,128]{3,2,1,0:T(8,128)S(1)}, f32[2,4,24,128]{3,2,1,0:T(8,128)S(1)}, u32[]{:S(2)}, u32[]{:S(2)}) collective-permute-start(f32[2,4,24,128]{3,2,1,0:T(8,128)S(1)} %get-tuple-element.69), channel_id=1, source_target_pairs={{0,16},{1,17},{2,18},{3,19},{4,20},{5,21},{6,22},{7,23},{8,24},{9,... | collective-permute-start | bytes 294920 | tf_op jit(solution)/shard_map/ppermute | solution.py:19
  109.8 11.1 %collective-permute-start.43 = (f32[2,4,24,128]{3,2,1,0:T(8,128)S(1)}, f32[2,4,24,128]{3,2,1,0:T(8,128)S(1)}, u32[]{:S(2)}, u32[]{:S(2)}) collective-permute-start(f32[2,4,24,128]{3,2,1,0:T(8,128)S(1)} %get-tuple-element.70), channel_id=1, source_target_pairs={{0,17},{1,16},{2,19},{3,18},{4,21},{5,20},{6,23},{7,22},{8,25},{9,... | collective-permute-start | bytes 294920 | tf_op jit(solution)/shard_map/ppermute | solution.py:19
  111.3 10.4 %collective-permute-start.37 = (f32[2,4,24,128]{3,2,1,0:T(8,128)S(1)}, f32[2,4,24,128]{3,2,1,0:T(8,128)S(1)}, u32[]{:S(2)}, u32[]{:S(2)}) collective-permute-start(f32[2,4,24,128]{3,2,1,0:T(8,128)S(1)} %get-tuple-element.62), channel_id=1, source_target_pairs={{0,1},{1,0},{2,3},{3,2},{4,5},{5,4},{6,7},{7,6},{8,9},{9,8},{10,11... | collective-permute-start | bytes 294920 | tf_op jit(solution)/shard_map/ppermute | solution.py:19
  111.8 9.9 %collective-permute-start.38 = (f32[2,4,24,128]{3,2,1,0:T(8,128)S(1)}, f32[2,4,24,128]{3,2,1,0:T(8,128)S(1)}, u32[]{:S(2)}, u32[]{:S(2)}) collective-permute-start(f32[2,4,24,128]{3,2,1,0:T(8,128)S(1)} %get-tuple-element.63), channel_id=1, source_target_pairs={{0,16},{1,17},{2,18},{3,19},{4,20},{5,21},{6,22},{7,23},{8,24},{9,... | collective-permute-start | bytes 294920 | tf_op jit(solution)/shard_map/ppermute | solution.py:19
  113.4 8.2 %collective-permute-start.39 = (f32[2,4,24,128]{3,2,1,0:T(8,128)S(1)}, f32[2,4,24,128]{3,2,1,0:T(8,128)S(1)}, u32[]{:S(2)}, u32[]{:S(2)}) collective-permute-start(f32[2,4,24,128]{3,2,1,0:T(8,128)S(1)} %get-tuple-element.64), channel_id=1, source_target_pairs={{0,17},{1,16},{2,19},{3,18},{4,21},{5,20},{6,23},{7,22},{8,25},{9,... | collective-permute-start | bytes 294920 | tf_op jit(solution)/shard_map/ppermute | solution.py:19
